TPU v7x, 32 devices: a whole 2x2x4 slice. The times are simulated.
32 devices in a mesh: walk: 4 (over y, x), pair: 8 (over z, core).
Axes of the slice: x: 2, y: 2, z: 4, core: 2. Of those that a mesh axis runs over, the one named last changes fastest.
Arguments:
- walkers: float32 [64, 64, 512], P(('walk', 'pair')), may hold values from -6 to 6
- inverse_intersection: float32 [64, 64, 64], P(('walk', 'pair')), may hold values from -0.75 to 0.75
- trial: bfloat16 [64, 512], P(None, 'walk'), may hold values from -0.095703125 to 0.095703125
- fields: float32 [64, 4096], P(('walk', 'pair')), may hold values from -6 to 6
- cholesky: bfloat16 [512, 512, 4096], P('pair', 'walk'), may hold values from -0.083984375 to 0.083984375
Outputs:
- advanced_walkers: float32 [64, 64, 512], P(('walk', 'pair'))
- log_importance: float32 [64], P(('walk', 'pair'))
All inputs are finite; a program needn't handle non-finite values.
Results may differ from a plain program's by a relative error of at most 0.011.
Values may be sent and summed in bfloat16 or wider, within the bound.
No kernel may reach another device: no remote copies, remote signals or barrier semaphores. Data moves between devices by JAX's collectives and lax.ppermute only.
A program may use at most 128 MiB of HBM per device.

v0:
```python
import jax
import jax.numpy as jnp
from jax import lax
from jax.sharding import PartitionSpec as P

time_root = 0.1


def per_device(walkers, inverse_intersection, trial, fields, cholesky):
    highest = lax.Precision.HIGHEST
    pair_count = lax.axis_size("pair")
    walk_count = lax.axis_size("walk")
    local_walkers, occupied, orbitals = walkers.shape
    block_rows = cholesky.shape[0]
    block_cols = cholesky.shape[1]
    vectors = cholesky.shape[2]
    flat_slab = cholesky.reshape(block_rows * block_cols, vectors)
    split_walkers = walkers.reshape(local_walkers, occupied, pair_count, block_rows)
    rotated = jnp.einsum("wji,wjbr->wbir", inverse_intersection, split_walkers, precision=highest)
    rotated = rotated.astype(jnp.bfloat16).reshape(local_walkers, pair_count, occupied * block_rows)
    regrouped = lax.all_to_all(rotated, "pair", split_axis=1, concat_axis=0, tiled=True)
    shard_piece = lax.all_gather(regrouped, "walk", axis=0, tiled=True)
    rows_here = shard_piece.shape[0]
    rotated_piece = shard_piece.reshape(rows_here, occupied, block_rows)
    greens = jnp.einsum("wir,iq->wrq", rotated_piece, trial, preferred_element_type=jnp.float32)
    greens = greens.astype(jnp.bfloat16).reshape(rows_here, block_rows * block_cols)
    partial_bias = jnp.dot(greens, flat_slab, preferred_element_type=jnp.float32)
    every_field = lax.all_gather(fields, ("walk", "pair"), axis=0, tiled=True)
    force_bias = lax.psum(partial_bias, ("walk", "pair"))
    bias_shift = -time_root * force_bias
    shifted = (every_field - bias_shift).astype(jnp.bfloat16)
    position = lax.axis_index(("walk", "pair")) * local_walkers
    own_shift = lax.dynamic_slice_in_dim(bias_shift, position, local_walkers, 0)
    log_importance = jnp.sum(fields * own_shift - 0.5 * own_shift * own_shift, axis=1)
    potential = lax.dot_general(
        shifted, flat_slab, (((1,), (1,)), ((), ())), preferred_element_type=jnp.float32
    )
    potential = potential.astype(jnp.bfloat16)
    blocks = potential.reshape(walk_count * pair_count, local_walkers, block_rows, block_cols)
    arrived = lax.all_to_all(blocks, ("walk", "pair"), split_axis=0, concat_axis=0, tiled=True)
    arrived = arrived.reshape(walk_count, pair_count, local_walkers, block_rows, block_cols)
    series_term = walkers
    summed = walkers
    for degree in range(1, 7):
        operand = series_term.astype(jnp.bfloat16).reshape(
            local_walkers, occupied, walk_count, block_cols
        )
        product = jnp.einsum(
            "kiac,abkrc->kibr", operand, arrived, preferred_element_type=jnp.float32
        )
        series_term = product.reshape(local_walkers, occupied, orbitals) * (-time_root / degree)
        summed = summed + series_term
    return (summed, log_importance)


def solution(mesh):
    in_specs = (
        P(("walk", "pair"), None, None),
        P(("walk", "pair"), None, None),
        P(None, "walk"),
        P(("walk", "pair"), None),
        P("pair", "walk", None),
    )
    out_specs = (P(("walk", "pair"), None, None), P(("walk", "pair")))
    return jax.shard_map(
        per_device, mesh=mesh, in_specs=in_specs, out_specs=out_specs, check_vma=False
    )
```

profile of v0, /device:TPU:0, one launch (start us, length us, event | category | flops | bytes accessed | tf_op | source)
XLA Modules:
  0.0 289.0 jit_solution(5728809208789449599)
XLA Ops:
  7.2 1.2 copy.100
  8.4 0.6 fusion.6
  9.0 0.2 copy.101
  9.1 0.9 reshape.93
  10.0 6.4 %all-to-all-start = ((bf16[2,8,4096]{2,0,1:T(2,128)(2,1)}), bf16[2,8,4096]{2,0,1:T(2,128)(2,1)S(1)}, u32[]{:S(2)}, u32[]{:S(2)}) async-start(bf16[2,8,4096]{2,0,1:T(2,128)(2,1)} %reshape.93), calls=%async_computation | async-start | bytes 262144 | tf_op jit(solution)/shard_map/all_to_all | solution.py:21
  16.4 0.7 all-gather.3.cloned.1.call-update
  17.2 6.0 %all-to-all-done = bf16[2,8,4096]{2,0,1:T(2,128)(2,1)S(1)} async-done(((bf16[2,8,4096]{2,0,1:T(2,128)(2,1)}), bf16[2,8,4096]{2,0,1:T(2,128)(2,1)S(1)}, u32[]{:S(2)}, u32[]{:S(2)}) %all-to-all-start) | async-done | bytes 131104 | tf_op jit(solution)/shard_map/all_to_all | solution.py:21
  23.1 0.1 all_to_all.19
  23.2 10.2 %all_gather.7 = bf16[64,1,4096]{2,0,1:T(8,128)(2,1)S(1)} all-gather(bf16[16,1,4096]{2,0,1:T(8,128)(2,1)S(1)} %all_to_all.19), channel_id=1, replica_groups=mesh['walk'=4,'pair'=8] {'walk'}, dimensions={0}, use_global_device_ids=true | all-gather | bytes 655360 | tf_op jit(solution)/shard_map/all_gather | solution.py:22
  33.4 1.1 reshape.71
  34.5 1.6 copy.62
  36.2 24.8 %convolution_bitcast_fusion = f32[64,4096]{1,0:T(8,128)} fusion(bf16[64,128,4096]{2,1,0:T(8,128)(2,1)} %param.9, bf16[64,64,64]{1,0,2:T(8,128)(2,1)S(1)} %copy.62, bf16[64,128]{1,0:T(8,128)(2,1)} %param.7), kind=kOutput, calls=%fused_computation.1 | convolution fusion | flops 4362600448 | bytes 68698112 | tf_op jit(solution)/shard_map/dot_general | solution.py:27
  61.0 14.5 %all-gather.3.cloned.1.call-done = f32[32,2,4096]{2,1,0:T(2,128)} async-done(((f32[1,2,4096]{2,1,0:T(2,128)}), f32[32,2,4096]{2,1,0:T(2,128)}) %all-gather.3.cloned.1.call-update) | async-done | bytes 1048592 | tf_op jit(solution)/shard_map/all_gather | solution.py:28
  75.5 1.9 reshape.77
  77.5 132.9 %all-reduce.2.cloned.1.call-done = f32[64,4096]{1,0:T(8,128)} async-done(((f32[64,4096]{1,0:T(8,128)}), f32[64,4096]{1,0:T(8,128)}) %all-reduce.2.cloned.1.call-update) | async-done | bytes 1048592 | tf_op jit(solution)/shard_map/psum | solution.py:29
  210.3 31.1 %fusion = bf16[8,8,64,128]{3,1,2,0:T(8,128)(2,1)S(1)} fusion(bf16[8192,4096]{1,0:T(8,128)(2,1)} %bitcast.9, f32[64,4096]{1,0:T(8,128)S(1)} %reshape.77, f32[64,4096]{1,0:T(8,128)} %all-reduce.2.cloned.1.call-done), kind=kOutput, calls=%fused_computation.3 | convolution fusion | flops 4296278016 | bytes 70254592 | tf_op jit(solution)/shard_map/dot_general | solution.py:35
  241.5 1.3 copy.118
  242.8 3.7 %all-to-all-start.1 = ((bf16[32,2,64,128]{3,2,1,0:T(8,128)(2,1)}), bf16[32,2,64,128]{3,2,1,0:T(8,128)(2,1)S(1)}, u32[]{:S(2)}, u32[]{:S(2)}) async-start(bf16[32,2,64,128]{3,2,1,0:T(8,128)(2,1)} %bitcast.106), calls=%async_computation.1 | async-start | bytes 2097152 | tf_op jit(solution)/shard_map/all_to_all | solution.py:40
  246.6 0.1 broadcast_multiply_fusion
  246.7 0.7 fusion.20
  247.4 26.4 %all-to-all-done.1 = bf16[32,2,64,128]{3,2,1,0:T(8,128)(2,1)S(1)} async-done(((bf16[32,2,64,128]{3,2,1,0:T(8,128)(2,1)}), bf16[32,2,64,128]{3,2,1,0:T(8,128)(2,1)S(1)}, u32[]{:S(2)}, u32[]{:S(2)}) %all-to-all-start.1) | async-done | bytes 1048608 | tf_op jit(solution)/shard_map/all_to_all | solution.py:40
  273.8 0.4 fusion.16
  274.2 0.1 bitcast_multiply_fusion
  274.3 0.2 copy.104
  274.5 0.6 fusion.24
  275.1 0.2 copy.70
  275.3 0.1 convert_element_type.66
  275.4 0.3 copy.69
  275.8 0.1 mul.100
  275.9 0.6 fusion.25
  276.5 0.2 copy.74
  276.7 0.1 convert_element_type.68
  276.9 0.3 copy.73
  277.2 0.1 mul.103
  277.3 0.6 fusion.26
  278.0 0.2 copy.78
  278.1 0.1 convert_element_type.70
  278.3 0.3 copy.77
  278.6 0.1 mul.106
  278.8 0.6 fusion.27
  279.4 0.2 copy.82
  279.6 0.1 convert_element_type.72
  279.7 0.6 fusion.1
  280.3 0.3 copy.85
  280.7 0.1 mul.112
  280.8 0.3 copy.81
  281.1 0.1 mul.109
  281.3 0.9 add_add_fusion
  (13 shorter events, 0.2 us)
Async XLA Ops:
  7.2 1.2 copy-start
  10.0 13.1 %all-to-all-start = ((bf16[2,8,4096]{2,0,1:T(2,128)(2,1)}), bf16[2,8,4096]{2,0,1:T(2,128)(2,1)S(1)}, u32[]{:S(2)}, u32[]{:S(2)}) async-start(bf16[2,8,4096]{2,0,1:T(2,128)(2,1)} %reshape.93), calls=%async_computation | async-start | bytes 262144 | tf_op jit(solution)/shard_map/all_to_all | solution.py:21
  16.4 59.1 %all-gather.3.cloned.1.call-start = ((), (), s32[]{:S(2)}) async-start(), calls=%async_computation.3 | async-start | bytes 1081344 | tf_op jit(solution)/shard_map/all_gather | solution.py:28
  17.1 193.2 %all-reduce.2.cloned.1.call-start = ((), (), s32[]{:S(2)}) async-start(), calls=%async_computation.2 | async-start | bytes 2097152 | tf_op jit(solution)/shard_map/psum | solution.py:29
  36.1 210.4 %copy-start.2 = (f32[2,64,512]{2,1,0:T(8,128)S(1)}, f32[2,64,512]{2,1,0:T(8,128)}, u32[]{:S(2)}) copy-start(f32[2,64,512]{2,1,0:T(8,128)} %param.5) | copy-start | bytes 786436
  36.2 210.6 %copy-start.3 = (f32[2,4096]{1,0:T(2,128)S(1)}, f32[2,4096]{1,0:T(2,128)}, u32[]{:S(2)}) copy-start(f32[2,4096]{1,0:T(2,128)} %param.8) | copy-start | bytes 98308
  210.3 36.3 %copy-start.1 = (f32[64,4096]{1,0:T(8,128)S(1)}, f32[64,4096]{1,0:T(8,128)}, u32[]{:S(2)}) copy-start(f32[64,4096]{1,0:T(8,128)} %all-reduce.2.cloned.1.call-done) | copy-start | bytes 3145732
  242.8 31.0 %all-to-all-start.1 = ((bf16[32,2,64,128]{3,2,1,0:T(8,128)(2,1)}), bf16[32,2,64,128]{3,2,1,0:T(8,128)(2,1)S(1)}, u32[]{:S(2)}, u32[]{:S(2)}) async-start(bf16[32,2,64,128]{3,2,1,0:T(8,128)(2,1)} %bitcast.106), calls=%async_computation.1 | async-start | bytes 2097152 | tf_op jit(solution)/shard_map/all_to_all | solution.py:40
Sparse Core Ops, SparseCore 0:
  20.2 55.2 all-gather.2
  80.7 129.6 all-reduce.1
where the time goes:
time: 289 us
  waiting for transfers between devices  180 us (62%)
  matrix products  60 us (21%)
  between operations  14.3 us (5%)
  local copies, waits for them, and re-layouts  12.1 us (4%)
  starting transfers between devices  10.2 us (4%)
  blocking collectives  10.2 us (4%)
    psum x1, waiting for transfers between devices, per_device(): force_bias = lax.psum(partial_bias, ('walk', 'pair'))  133 us
    dot_general x1, matrix products, per_device(): lax.dot_general(shifted, flat_slab, (((1,), (1,)), ((), ())), preferred_e...  31.1 us
    all_to_all x1, waiting for transfers between devices, per_device(): lax.all_to_all(blocks, ('walk', 'pair'), split_axis=0, concat_axis=0, til...  26.4 us
    dot_general x1, matrix products, per_device(): jnp.dot(greens, flat_slab, preferred_element_type=jnp.float32)  24.8 us
    all_gather x1, waiting for transfers between devices, per_device(): every_field = lax.all_gather(fields, ('walk', 'pair'), axis=0, tiled=True)  14.5 us
    all_gather x1, blocking collectives, per_device(): shard_piece = lax.all_gather(regrouped, 'walk', axis=0, tiled=True)  10.2 us
    all_to_all x1, starting transfers between devices, per_device(): lax.all_to_all(rotated, 'pair', split_axis=1, concat_axis=0, tiled=True)  6.35 us
    all_to_all x1, waiting for transfers between devices, per_device(): lax.all_to_all(rotated, 'pair', split_axis=1, concat_axis=0, tiled=True)  5.97 us
  transfers between devices with their start and end apart: 4, of which 4 were waited for; matrix products, arithmetic and copies ran while one was open for 11% of the time, Pallas kernels for 0%

commit v1 on v0

--- a/solution.py
+++ b/solution.py
@@ -25,13 +25,18 @@
     greens = jnp.einsum("wir,iq->wrq", rotated_piece, trial, preferred_element_type=jnp.float32)
     greens = greens.astype(jnp.bfloat16).reshape(rows_here, block_rows * block_cols)
     partial_bias = jnp.dot(greens, flat_slab, preferred_element_type=jnp.float32)
-    every_field = lax.all_gather(fields, ("walk", "pair"), axis=0, tiled=True)
-    force_bias = lax.psum(partial_bias, ("walk", "pair"))
-    bias_shift = -time_root * force_bias
-    shifted = (every_field - bias_shift).astype(jnp.bfloat16)
-    position = lax.axis_index(("walk", "pair")) * local_walkers
-    own_shift = lax.dynamic_slice_in_dim(bias_shift, position, local_walkers, 0)
+    rows_walk = rows_here // walk_count
+    outgoing = partial_bias.astype(jnp.bfloat16).reshape(walk_count, rows_walk, vectors)
+    incoming = lax.all_to_all(outgoing, "walk", split_axis=0, concat_axis=0, tiled=True)
+    walk_sum = jnp.sum(incoming.astype(jnp.float32), axis=0)
+    outgoing = walk_sum.astype(jnp.bfloat16).reshape(pair_count, local_walkers, vectors)
+    incoming = lax.all_to_all(outgoing, "pair", split_axis=0, concat_axis=0, tiled=True)
+    force_bias = jnp.sum(incoming.astype(jnp.float32), axis=0)
+    own_shift = -time_root * force_bias
     log_importance = jnp.sum(fields * own_shift - 0.5 * own_shift * own_shift, axis=1)
+    own_shifted = (fields - own_shift).astype(jnp.bfloat16)
+    pair_shifted = lax.all_gather(own_shifted, "pair", axis=0, tiled=True)
+    shifted = lax.all_gather(pair_shifted, "walk", axis=0, tiled=True)
     potential = lax.dot_general(
         shifted, flat_slab, (((1,), (1,)), ((), ())), preferred_element_type=jnp.float32
     )

time: 289 us -> 165 us (0.57)
  waiting for transfers between devices: 180 us -> 27.2 us
  blocking collectives: 10.2 us -> 65.7 us
  between operations: 14.3 us -> 0.93 us
  starting transfers between devices: 10.2 us -> 2.92 us
  matrix products: 60 us -> 56.8 us
    psum x1 -> x0, waiting for transfers between devices: 133 us -> none  [per_device(): force_bias = lax.psum(partial_bias, ('walk', 'pair'))]
    all_to_all x0 -> x3, blocking collectives: none -> 32 us  [the longest x1 12.9 us: per_device(): lax.all_to_all(rotated, 'pair', split_axis=1, concat_axis=0, tiled=True)]
    all_gather x0 -> x2, blocking collectives: none -> 23.7 us  [the longest x1 13.9 us: per_device(): pair_shifted = lax.all_gather(own_shifted, 'pair', axis=0, tiled=True)]
    all_gather x1 -> x0, waiting for transfers between devices: 14.5 us -> none  [per_device(): every_field = lax.all_gather(fields, ('walk', 'pair'), axis=0, tiled=True)]
    all_to_all x1 -> x0, starting transfers between devices: 6.35 us -> none  [per_device(): lax.all_to_all(rotated, 'pair', split_axis=1, concat_axis=0, tiled=True)]
    all_to_all x1 -> x0, waiting for transfers between devices: 5.97 us -> none  [per_device(): lax.all_to_all(rotated, 'pair', split_axis=1, concat_axis=0, tiled=True)]
  transfers between devices with their start and end apart: 4 -> 1, of which waited for: 4 -> 1; matrix products, arithmetic and copies ran while one was open for 11% -> 0% of each run, Pallas kernels for 0% -> 0%
where the time goes in v1:
time: 165 us
  blocking collectives  65.7 us (40%)
  matrix products  56.8 us (34%)
  waiting for transfers between devices  27.2 us (16%)
  local copies, waits for them, and re-layouts  9.58 us (6%)
  starting transfers between devices  2.92 us (2%)
  other arithmetic  1.9 us (1%)
    dot_general x1, matrix products, per_device(): lax.dot_general(shifted, flat_slab, (((1,), (1,)), ((), ())), preferred_e...  28.9 us
    all_to_all x1, waiting for transfers between devices, per_device(): lax.all_to_all(blocks, ('walk', 'pair'), split_axis=0, concat_axis=0, til...  27.2 us
    dot_general x1, matrix products, per_device(): jnp.dot(greens, flat_slab, preferred_element_type=jnp.float32)  23.8 us
    all_gather x1, blocking collectives, per_device(): pair_shifted = lax.all_gather(own_shifted, 'pair', axis=0, tiled=True)  13.9 us
    all_to_all x1, blocking collectives, per_device(): lax.all_to_all(rotated, 'pair', split_axis=1, concat_axis=0, tiled=True)  12.9 us
    all_gather x1, blocking collectives, per_device(): shard_piece = lax.all_gather(regrouped, 'walk', axis=0, tiled=True)  10 us
    all_to_all x1, blocking collectives, per_device(): lax.all_to_all(outgoing, 'walk', split_axis=0, concat_axis=0, tiled=True)  9.92 us
    all_gather x1, blocking collectives, per_device(): shifted = lax.all_gather(pair_shifted, 'walk', axis=0, tiled=True)  9.71 us
  transfers between devices with their start and end apart: 1, of which 1 were waited for; matrix products, arithmetic and copies ran while one was open for 0% of the time, Pallas kernels for 0%

profile of v1, /device:TPU:0, one launch (start us, length us, event | category | flops | bytes accessed | tf_op | source)
XLA Modules:
  0.0 165.0 jit_solution(17718990606001667348)
XLA Ops:
  0.7 1.2 copy.209
  1.8 0.6 fusion.7
  2.4 0.2 copy.210
  2.6 0.2 reshape.101
  2.9 12.9 %all_to_all.33 = bf16[2,8,4096]{2,0,1:T(2,128)(2,1)S(1)} all-to-all(bf16[2,8,4096]{2,0,1:T(2,128)(2,1)S(1)} %reshape.101), channel_id=1, replica_groups=mesh['walk'=4,'pair'=8] {'pair'}, dimensions={1} | all-to-all | bytes 262144 | tf_op jit(solution)/shard_map/all_to_all | solution.py:21
  15.8 10.0 %all_gather.9 = bf16[64,1,4096]{2,0,1:T(8,128)(2,1)S(1)} all-gather(bf16[16,1,4096]{2,0,1:T(8,128)(2,1)S(1)} %all_to_all.25), channel_id=1, replica_groups=mesh['walk'=4,'pair'=8] {'walk'}, dimensions={0}, use_global_device_ids=true | all-gather | bytes 655360 | tf_op jit(solution)/shard_map/all_gather | solution.py:22
  25.9 1.1 reshape.77
  27.0 1.6 copy.170
  28.7 23.8 %fusion = bf16[64,4096]{1,0:T(8,128)(2,1)S(1)} fusion(bf16[64,128,4096]{2,1,0:T(8,128)(2,1)} %param.9, bf16[64,64,64]{1,0,2:T(8,128)(2,1)S(1)} %copy.170, bf16[64,128]{1,0:T(8,128)(2,1)} %param.7), kind=kOutput, calls=%fused_computation.2 | convolution fusion | flops 4362862592 | bytes 68173824 | tf_op jit(solution)/shard_map/dot_general | solution.py:27
  52.5 9.9 %all_to_all.34 = bf16[4,16,4096]{2,1,0:T(8,128)(2,1)S(1)} all-to-all(bf16[4,16,4096]{2,1,0:T(8,128)(2,1)S(1)} %bitcast.111), channel_id=1, replica_groups=mesh['walk'=4,'pair'=8] {'walk'}, dimensions={0} | all-to-all | bytes 1048576 | tf_op jit(solution)/shard_map/all_to_all | solution.py:30
  62.4 0.1 reduce_sum.30
  62.5 0.1 reshape.79
  62.6 9.2 %all_to_all.35 = bf16[8,2,4096]{2,1,0:T(2,128)(2,1)S(1)} all-to-all(bf16[8,2,4096]{2,1,0:T(2,128)(2,1)S(1)} %reshape.79), channel_id=1, replica_groups=mesh['walk'=4,'pair'=8] {'pair'}, dimensions={0} | all-to-all | bytes 262144 | tf_op jit(solution)/shard_map/all_to_all | solution.py:33
  71.7 0.2 convert_reduce_fusion
  71.9 0.7 subtract_reduce_fusion
  72.6 13.9 %all-gather = bf16[8,2,4096]{2,1,0:T(2,128)(2,1)S(1)} all-gather(bf16[1,2,4096]{2,1,0:T(2,128)(2,1)S(1)} %get-tuple-element.5), channel_id=1, replica_groups=mesh['walk'=4,'pair'=8] {'pair'}, dimensions={0}, use_global_device_ids=true | all-gather | bytes 147456 | tf_op jit(solution)/shard_map/all_gather | solution.py:38
  86.6 9.7 %all_gather.11 = bf16[64,4096]{1,0:T(8,128)(2,1)S(1)} all-gather(bf16[16,4096]{1,0:T(8,128)(2,1)S(1)} %reshape.85), channel_id=1, replica_groups=mesh['walk'=4,'pair'=8] {'walk'}, dimensions={0}, use_global_device_ids=true | all-gather | bytes 655360 | tf_op jit(solution)/shard_map/all_gather | solution.py:39
  96.3 28.9 %fusion.1 = bf16[8,8,64,128]{3,1,2,0:T(8,128)(2,1)S(1)} fusion(bf16[64,4096]{1,0:T(8,128)(2,1)S(1)} %all_gather.11, bf16[8192,4096]{1,0:T(8,128)(2,1)} %bitcast.10), kind=kOutput, calls=%fused_computation.4 | convolution fusion | flops 4295491584 | bytes 68681728 | tf_op jit(solution)/shard_map/dot_general | solution.py:40
  125.2 1.3 copy.227
  126.5 2.9 %all-to-all-start.3 = ((bf16[32,2,64,128]{3,2,1,0:T(8,128)(2,1)}), bf16[32,2,64,128]{3,2,1,0:T(8,128)(2,1)S(1)}, u32[]{:S(2)}, u32[]{:S(2)}) async-start(bf16[32,2,64,128]{3,2,1,0:T(8,128)(2,1)} %bitcast.46), calls=%async_computation.3 | async-start | bytes 2097152 | tf_op jit(solution)/shard_map/all_to_all | solution.py:45
  129.5 27.2 %all-to-all-done.3 = bf16[32,2,64,128]{3,2,1,0:T(8,128)(2,1)S(1)} async-done(((bf16[32,2,64,128]{3,2,1,0:T(8,128)(2,1)}), bf16[32,2,64,128]{3,2,1,0:T(8,128)(2,1)S(1)}, u32[]{:S(2)}, u32[]{:S(2)}) %all-to-all-start.3) | async-done | bytes 1048608 | tf_op jit(solution)/shard_map/all_to_all | solution.py:45
  156.7 0.4 fusion.17
  157.1 0.1 bitcast_multiply_fusion
  157.2 0.2 copy.213
  157.4 0.6 fusion.25
  158.0 0.2 copy.179
  158.2 0.1 convert_element_type.76
  158.3 0.3 copy.178
  158.6 0.1 mul.94
  158.8 0.6 fusion.26
  159.4 0.2 copy.183
  159.6 0.1 convert_element_type.78
  159.8 0.3 copy.182
  160.1 0.1 mul.97
  160.2 0.6 fusion.27
  160.8 0.2 copy.187
  161.0 0.1 convert_element_type.80
  161.2 0.3 copy.186
  161.5 0.1 mul.100
  161.6 0.6 fusion.28
  162.3 0.2 copy.191
  162.4 0.1 convert_element_type.82
  162.6 0.6 fusion.2
  163.2 0.3 copy.194
  163.5 0.1 mul.106
  163.7 0.3 copy.190
  164.0 0.1 mul.103
  164.1 0.9 add_add_fusion
  (10 shorter events, 0.2 us)
Async XLA Ops:
  0.6 1.2 copy-start
  0.6 71.2 %copy-start.2 = (f32[2,4096]{1,0:T(2,128)S(1)}, f32[2,4096]{1,0:T(2,128)}, u32[]{:S(2)}) copy-start(f32[2,4096]{1,0:T(2,128)} %param.8) | copy-start | bytes 98308
  28.6 100.8 %copy-start.1 = (f32[2,64,512]{2,1,0:T(8,128)S(1)}, f32[2,64,512]{2,1,0:T(8,128)}, u32[]{:S(2)}) copy-start(f32[2,64,512]{2,1,0:T(8,128)} %param.5) | copy-start | bytes 786436
  126.5 30.2 %all-to-all-start.3 = ((bf16[32,2,64,128]{3,2,1,0:T(8,128)(2,1)}), bf16[32,2,64,128]{3,2,1,0:T(8,128)(2,1)S(1)}, u32[]{:S(2)}, u32[]{:S(2)}) async-start(bf16[32,2,64,128]{3,2,1,0:T(8,128)(2,1)} %bitcast.46), calls=%async_computation.3 | async-start | bytes 2097152 | tf_op jit(solution)/shard_map/all_to_all | solution.py:45

commit v2 on v1

--- a/solution.py
+++ b/solution.py
@@ -1,13 +1,413 @@
+import functools
+
 import jax
 import jax.numpy as jnp
 from jax import lax
+from jax.experimental import pallas as pl
+from jax.experimental.pallas import tpu as pltpu
 from jax.sharding import PartitionSpec as P
 
 time_root = 0.1
-
-
-def per_device(walkers, inverse_intersection, trial, fields, cholesky):
-    highest = lax.Precision.HIGHEST
+lanes = 128
+tile_rows = 512
+row_group = 16
+ring_slots = 2
+ahead = 3
+stream_slots = 4
+
+mebi = 1 << 20
+grant = 14 * mebi
+highest = lax.Precision.HIGHEST
+whole = pl.BlockSpec(memory_space=pltpu.VMEM)
+anywhere = pl.BlockSpec(memory_space=pltpu.HBM)
+scalar = pl.BlockSpec(memory_space=pltpu.SMEM)
+
+
+def in_hbm(array):
+    return pltpu.with_memory_space_constraint(array, pltpu.HBM)
+
+
+def rotate_kernel(walkers_hbm, inverse_hbm, out_ref, walkers_ref, inverse_ref, sem):
+    copies = [
+        pltpu.make_async_copy(walkers_hbm, walkers_ref, sem.at[0]),
+        pltpu.make_async_copy(inverse_hbm, inverse_ref, sem.at[1]),
+    ]
+    for copy in copies:
+        copy.start()
+    for copy in copies:
+        copy.wait()
+    count, occupied, orbitals = walkers_ref.shape
+    half = out_ref.shape[1] // count
+    pairs = orbitals // half // 2
+    for w in range(count):
+        turned = lax.dot_general(
+            walkers_ref[w], inverse_ref[w], (((0,), (0,)), ((), ())),
+            precision=highest, preferred_element_type=jnp.float32,
+        )
+        for b in range(pairs):
+            low = turned[2 * b * half : (2 * b + 1) * half]
+            high = turned[(2 * b + 1) * half : (2 * b + 2) * half]
+            both = jnp.concatenate([low, high], axis=1).astype(jnp.bfloat16)
+            for a in range(out_ref.shape[0] // pairs):
+                out_ref[a * pairs + b, w * half : (w + 1) * half, :] = both
+
+
+def rotate(walkers, inverse, walks, pairs):
+    count, occupied, orbitals = walkers.shape
+    half = orbitals // pairs // 2
+    return pl.pallas_call(
+        rotate_kernel,
+        out_shape=jax.ShapeDtypeStruct(
+            (walks * pairs, count * half, 2 * occupied), jnp.bfloat16
+        ),
+        in_specs=[anywhere, anywhere],
+        out_specs=whole,
+        scratch_shapes=[
+            pltpu.VMEM(walkers.shape, jnp.float32),
+            pltpu.VMEM(inverse.shape, jnp.float32),
+            pltpu.SemaphoreType.DMA((2,)),
+        ],
+        compiler_params=pltpu.CompilerParams(vmem_limit_bytes=8 * mebi),
+        name="rotate",
+    )(in_hbm(walkers), in_hbm(inverse))
+
+
+def bias_kernel(core_ref, rotated_ref, trial_ref, slab_ref, own_ref, sent_ref, kept_ref, wide, rows, greens, total, ring, kept_sem, ring_sem):
+    vectors = total.shape[1]
+    walkers_all = total.shape[0]
+    half = rotated_ref.shape[0] // walkers_all
+    occupied, columns = trial_ref.shape
+    kept_tiles = kept_ref.shape[0] // tile_rows
+    tiles = slab_ref.shape[0] // tile_rows
+    blocks = vectors // lanes
+
+    def kept_copy(t):
+        span = pl.ds(pl.multiple_of(t * tile_rows, tile_rows), tile_rows)
+        return pltpu.make_async_copy(slab_ref.at[span], kept_ref.at[span], kept_sem.at[t])
+
+    def ring_copy(t):
+        slot = lax.rem(t - kept_tiles, ring_slots)
+        span = pl.ds(pl.multiple_of(t * tile_rows, tile_rows), tile_rows)
+        return pltpu.make_async_copy(slab_ref.at[span], ring.at[slot], ring_sem.at[slot])
+
+    for t in range(min(ahead, kept_tiles)):
+        kept_copy(t).start()
+    wide[: rotated_ref.shape[0], :] = rotated_ref[...].astype(jnp.float32)
+    for r in range(half):
+        rows[r * walkers_all : (r + 1) * walkers_all, :] = wide[
+            pl.ds(r, walkers_all, stride=half), :
+        ].astype(jnp.bfloat16)
+    nothing = jnp.zeros((occupied, columns), jnp.bfloat16)
+    trial = trial_ref[...]
+    double = jnp.concatenate(
+        [jnp.concatenate([trial, nothing], axis=1), jnp.concatenate([nothing, trial], axis=1)],
+        axis=0,
+    )
+    step = 8
+    for r0 in range(0, half, step):
+        product = jnp.dot(
+            rows[r0 * walkers_all : (r0 + step) * walkers_all, :], double,
+            preferred_element_type=jnp.float32,
+        ).astype(jnp.bfloat16)
+        for r in range(step):
+            piece = product[r * walkers_all : (r + 1) * walkers_all]
+            first = (r0 + r) * columns
+            second = (half + r0 + r) * columns
+            greens[:, first : first + columns] = piece[:, :columns]
+            greens[:, second : second + columns] = piece[:, columns:]
+    total[...] = jnp.zeros_like(total)
+
+    @pl.loop(0, kept_tiles)
+    def _(t):
+        start = pl.multiple_of(t * tile_rows, tile_rows)
+        coming = t + ahead
+
+        @pl.when(coming < kept_tiles)
+        def _():
+            kept_copy(coming).start()
+
+        @pl.when((coming >= kept_tiles) & (coming < min(kept_tiles + ring_slots, tiles)))
+        def _():
+            ring_copy(coming).start()
+
+        kept_copy(t).wait()
+        total[...] += jnp.dot(
+            greens[:, pl.ds(start, tile_rows)], kept_ref[pl.ds(start, tile_rows), :],
+            preferred_element_type=jnp.float32,
+        )
+
+    @pl.loop(kept_tiles, tiles)
+    def _(t):
+        start = pl.multiple_of(t * tile_rows, tile_rows)
+        slot = lax.rem(t - kept_tiles, ring_slots)
+        ring_copy(t).wait()
+        total[...] += jnp.dot(
+            greens[:, pl.ds(start, tile_rows)], ring[slot],
+            preferred_element_type=jnp.float32,
+        )
+
+        @pl.when(t + ring_slots < tiles)
+        def _():
+            ring_copy(t + ring_slots).start()
+
+    for j in range(blocks):
+        wide[j * walkers_all : (j + 1) * walkers_all, :] = total[:, j * lanes : (j + 1) * lanes]
+    local_walkers = own_ref.shape[1] // blocks
+    core = core_ref[0]
+    for g in range(own_ref.shape[0]):
+        for w in range(local_walkers):
+            for ref, side in ((own_ref, core), (sent_ref, 1 - core)):
+                row = (2 * g + side) * local_walkers + w
+                ref[g, w * blocks : (w + 1) * blocks, :] = wide[
+                    pl.ds(row, blocks, stride=walkers_all), :
+                ].astype(jnp.bfloat16)
+
+
+def bias_partial(core, local_walkers, rotated, trial, slab, walkers_all, kept_tiles):
+    vectors = slab.shape[1]
+    pairs = slab.shape[0]
+    half_shape = (
+        walkers_all // local_walkers // 2, local_walkers * vectors // lanes, lanes
+    )
+    height = max(rotated.shape[0], walkers_all * vectors // lanes)
+    return pl.pallas_call(
+        bias_kernel,
+        out_shape=(
+            jax.ShapeDtypeStruct(half_shape, jnp.bfloat16),
+            jax.ShapeDtypeStruct(half_shape, jnp.bfloat16),
+            pltpu.VMEM((kept_tiles * tile_rows, vectors), jnp.bfloat16),
+        ),
+        in_specs=[scalar, whole, whole, anywhere],
+        out_specs=(whole, whole, whole),
+        scratch_shapes=[
+            pltpu.VMEM((height, lanes), jnp.float32),
+            pltpu.VMEM(rotated.shape, jnp.bfloat16),
+            pltpu.VMEM((walkers_all, pairs), jnp.bfloat16),
+            pltpu.VMEM((walkers_all, vectors), jnp.float32),
+            pltpu.VMEM((ring_slots, tile_rows, vectors), jnp.bfloat16),
+            pltpu.SemaphoreType.DMA((kept_tiles,)),
+            pltpu.SemaphoreType.DMA((ring_slots,)),
+        ],
+        compiler_params=pltpu.CompilerParams(vmem_limit_bytes=grant),
+        cost_estimate=pl.CostEstimate(
+            flops=2 * walkers_all * slab.size, bytes_accessed=2 * slab.size, transcendentals=0
+        ),
+        name="bias_partial",
+    )(core, rotated, trial, slab)
+
+
+def add_kernel(own_ref, other_ref, out_ref):
+    added = own_ref[...].astype(jnp.float32) + other_ref[...].astype(jnp.float32)
+    out_ref[...] = added.astype(jnp.bfloat16)
+
+
+def add(own, other):
+    return pl.pallas_call(
+        add_kernel,
+        out_shape=jax.ShapeDtypeStruct(own.shape, jnp.bfloat16),
+        in_specs=[whole, whole],
+        out_specs=whole,
+        compiler_params=pltpu.CompilerParams(vmem_limit_bytes=4 * mebi),
+        name="add",
+    )(own, other)
+
+
+def shift_kernel(in_ref, fields_ref, copies_ref, log_ref, turned):
+    count, rows, _ = in_ref.shape
+    local_walkers, vectors = fields_ref.shape
+    blocks = vectors // lanes
+    added = in_ref[0].astype(jnp.float32)
+    for s in range(1, count):
+        added = added + in_ref[s].astype(jnp.float32)
+    bias_shift = -time_root * added
+    for j in range(blocks):
+        turned[j * local_walkers : (j + 1) * local_walkers, :] = fields_ref[
+            :, j * lanes : (j + 1) * lanes
+        ]
+    for w in range(local_walkers):
+        span = slice(w * blocks, (w + 1) * blocks)
+        own = turned[pl.ds(w, blocks, stride=local_walkers), :]
+        shift = bias_shift[span]
+        shifted = (own - shift).astype(jnp.bfloat16)
+        for s in range(copies_ref.shape[0]):
+            copies_ref[s, span, :] = shifted
+        score = jnp.sum(own * shift - 0.5 * shift * shift, axis=0, keepdims=True)
+        log_ref[w : w + 1, :] = jnp.broadcast_to(
+            jnp.sum(score, axis=1, keepdims=True), (1, lanes)
+        )
+
+
+def shift(incoming, fields):
+    count, rows, _ = incoming.shape
+    local_walkers = fields.shape[0]
+    return pl.pallas_call(
+        shift_kernel,
+        out_shape=(
+            jax.ShapeDtypeStruct((count, rows, lanes), jnp.bfloat16),
+            jax.ShapeDtypeStruct((local_walkers, lanes), jnp.float32),
+        ),
+        in_specs=[whole, whole],
+        out_specs=(whole, whole),
+        scratch_shapes=[pltpu.VMEM((rows, lanes), jnp.float32)],
+        compiler_params=pltpu.CompilerParams(vmem_limit_bytes=4 * mebi),
+        name="shift",
+    )(incoming, fields)
+
+
+def potential_kernel(kept_tiles, core_ref, own_ref, other_ref, kept_ref, slab_ref, out_ref, wide, shifted, product, ring, ring_sem):
+    half_rows = own_ref.shape[0]
+    walkers_all, vectors = shifted.shape
+    local_walkers = walkers_all // out_ref.shape[0]
+    blocks = vectors // lanes
+    tiles = slab_ref.shape[0] // tile_rows
+    per_tile = tile_rows // lanes
+    group = row_group // per_tile
+    core = core_ref[0]
+
+    def ring_copy(t):
+        slot = (t - kept_tiles) % ring_slots
+        span = pl.ds(t * tile_rows, tile_rows)
+        return pltpu.make_async_copy(slab_ref.at[span], ring.at[slot], ring_sem.at[slot])
+
+    for t in range(kept_tiles, min(kept_tiles + ring_slots, tiles)):
+        ring_copy(t).start()
+    wide[:half_rows, :] = own_ref[...].astype(jnp.float32)
+    wide[half_rows:, :] = other_ref[...].astype(jnp.float32)
+    for j in range(blocks):
+        shifted[:, j * lanes : (j + 1) * lanes] = wide[
+            pl.ds(j, walkers_all, stride=blocks), :
+        ].astype(jnp.bfloat16)
+    for t in range(tiles):
+        if t < kept_tiles:
+            tile = kept_ref[t * tile_rows : (t + 1) * tile_rows, :]
+        else:
+            ring_copy(t).wait()
+            tile = ring[(t - kept_tiles) % ring_slots]
+        values = lax.dot_general(
+            shifted[...], tile, (((1,), (1,)), ((), ())), preferred_element_type=jnp.float32
+        )
+        if t >= kept_tiles and t + ring_slots < tiles:
+            ring_copy(t + ring_slots).start()
+        place = t % group * per_tile
+        for r in range(per_tile):
+            product[(place + r) * walkers_all : (place + r + 1) * walkers_all, :] = values[
+                :, r * lanes : (r + 1) * lanes
+            ]
+        if t % group == group - 1:
+            base = t // group * row_group
+            for m in range(walkers_all):
+                side, rest = divmod(m, walkers_all // 2)
+                g, w = divmod(rest, local_walkers)
+                owner = 2 * g + (core if side == 0 else 1 - core)
+                out_ref[owner, w, base : base + row_group, :] = product[
+                    pl.ds(m, row_group, stride=walkers_all), :
+                ].astype(jnp.bfloat16)
+
+
+def potential(core, local_walkers, own, other, kept, slab, kept_tiles):
+    vectors = slab.shape[1]
+    walkers_all = 2 * own.shape[0] * lanes // vectors
+    rows = slab.shape[0] // lanes
+    return pl.pallas_call(
+        functools.partial(potential_kernel, kept_tiles),
+        out_shape=jax.ShapeDtypeStruct(
+            (walkers_all // local_walkers, local_walkers, rows, lanes), jnp.bfloat16
+        ),
+        in_specs=[scalar, whole, whole, whole, anywhere],
+        out_specs=whole,
+        scratch_shapes=[
+            pltpu.VMEM((2 * own.shape[0], lanes), jnp.float32),
+            pltpu.VMEM((walkers_all, vectors), jnp.bfloat16),
+            pltpu.VMEM((row_group * walkers_all, lanes), jnp.float32),
+            pltpu.VMEM((ring_slots, tile_rows, vectors), jnp.bfloat16),
+            pltpu.SemaphoreType.DMA((ring_slots,)),
+        ],
+        compiler_params=pltpu.CompilerParams(vmem_limit_bytes=grant),
+        cost_estimate=pl.CostEstimate(
+            flops=2 * walkers_all * slab.size, bytes_accessed=2 * slab.size, transcendentals=0
+        ),
+        name="potential",
+    )(core, own, other, pltpu.with_memory_space_constraint(kept, pltpu.VMEM), slab)
+
+
+def series_kernel(walk_count, walkers_ref, *refs):
+    pieces, out_ref, matrix = refs[:-2], refs[-2], refs[-1]
+    local_walkers, occupied, orbitals = walkers_ref.shape
+    pair_count = pieces[0].shape[0] // walk_count
+    block_rows = orbitals // pair_count
+    for w in range(local_walkers):
+        at = 0
+        for piece in pieces:
+            rows = piece.shape[2]
+            for a in range(walk_count):
+                for b in range(pair_count):
+                    top = b * block_rows + at
+                    matrix[w, top : top + rows, a * lanes : (a + 1) * lanes] = piece[
+                        a * pair_count + b, w
+                    ]
+            at += rows
+    terms = [walkers_ref[w] for w in range(local_walkers)]
+    sums = list(terms)
+    for degree in range(1, 7):
+        for w in range(local_walkers):
+            terms[w] = lax.dot_general(
+                terms[w].astype(jnp.bfloat16), matrix[w], (((1,), (1,)), ((), ())),
+                preferred_element_type=jnp.float32,
+            ) * (-time_root / degree)
+            sums[w] = sums[w] + terms[w]
+    for w in range(local_walkers):
+        out_ref[w] = sums[w]
+
+
+def series(walkers, pieces, walk_count):
+    local_walkers, occupied, orbitals = walkers.shape
+    return pl.pallas_call(
+        functools.partial(series_kernel, walk_count),
+        out_shape=jax.ShapeDtypeStruct(walkers.shape, jnp.float32),
+        in_specs=[whole] * (1 + len(pieces)),
+        out_specs=whole,
+        scratch_shapes=[pltpu.VMEM((local_walkers, orbitals, orbitals), jnp.bfloat16)],
+        compiler_params=pltpu.CompilerParams(vmem_limit_bytes=16 * mebi),
+        name="series",
+    )(walkers, *pieces)
+
+
+kept_share = 0.6875
+
+
+def fast(walkers, inverse_intersection, trial, fields, cholesky):
+    pair_count = lax.axis_size("pair")
+    walk_count = lax.axis_size("walk")
+    device_count = walk_count * pair_count
+    local_walkers, occupied, orbitals = walkers.shape
+    walkers_all = local_walkers * device_count
+    vectors = cholesky.shape[2]
+    blocks = vectors // lanes
+    slab = cholesky.reshape(-1, vectors)
+    tiles = slab.shape[0] // tile_rows
+    kept_tiles = int(tiles * kept_share)
+    everyone = ("walk", "pair")
+    exchange = functools.partial(
+        lax.all_to_all, axis_name=everyone, split_axis=0, concat_axis=0, tiled=True
+    )
+    rotated = rotate(walkers, inverse_intersection, walk_count, pair_count)
+    pieces = exchange(rotated).reshape(-1, 2 * occupied)
+    place = lax.axis_index("pair")
+    core = lax.rem(place, 2).reshape(1)
+    swap = [(i, i ^ 1) for i in range(pair_count)]
+    alike = [list(range(c, device_count, 2)) for c in range(2)]
+    own, sent, kept = bias_partial(
+        core, local_walkers, pieces, trial, slab, walkers_all, kept_tiles
+    )
+    incoming = exchange(add(own, lax.ppermute(sent, "pair", swap)), axis_index_groups=alike)
+    copies, log_rows = shift(incoming, fields)
+    own = exchange(copies, axis_index_groups=alike).reshape(-1, lanes)
+    other = lax.ppermute(own, "pair", swap)
+    arrived = [exchange(potential(core, local_walkers, own, other, kept, slab, kept_tiles))]
+    return (series(walkers, arrived, walk_count), log_rows[:, 0])
+
+
+def plain(walkers, inverse_intersection, trial, fields, cholesky):
     pair_count = lax.axis_size("pair")
     walk_count = lax.axis_size("walk")
     local_walkers, occupied, orbitals = walkers.shape
@@ -57,6 +457,18 @@
         summed = summed + series_term
     return (summed, log_importance)
 
+def per_device(walkers, inverse_intersection, trial, fields, cholesky):
+    block_rows, block_cols, vectors = cholesky.shape
+    fits = (
+        block_cols == lanes
+        and vectors % lanes == 0
+        and 2 * walkers.shape[1] == lanes
+        and block_rows % 32 == 0
+        and lax.axis_size("pair") % 2 == 0
+    )
+    step = fast if fits else plain
+    return step(walkers, inverse_intersection, trial, fields, cholesky)
+
 
 def solution(mesh):
     in_specs = (

time: 165 us -> 143 us (0.87)
  matrix products: 56.8 us -> 0 us
  Pallas kernels: 0 us -> 55.6 us
  blocking collectives: 65.7 us -> 26.8 us
  waiting for transfers between devices: 27.2 us -> 46.2 us
  starting transfers between devices: 2.92 us -> 10.2 us
  local copies, waits for them, and re-layouts: 9.58 us -> 3.08 us
  other arithmetic: 1.9 us -> 0 us
    dot_general x9 -> x0, matrix products: 56.8 us -> none  [the longest x1 28.9 us: per_device(): lax.dot_general(shifted, flat_slab, (((1,), (1,)), ((), ())), preferred_e...]
    pallas_call x0 -> x6, Pallas kernels: none -> 55.6 us  [the longest x1 25.1 us: bias_partial(): pl.pallas_call(bias_kernel, out_shape=(jax.ShapeDtypeStruct(half_shape, j...]
    all_gather x3 -> x0, blocking collectives: 33.7 us -> none  [the longest x1 13.9 us: per_device(): pair_shifted = lax.all_gather(own_shifted, 'pair', axis=0, tiled=True)]
    all_to_all x1 -> x2, waiting for transfers between devices: 27.2 us -> 43.1 us  [the longest x1 26.8 us: fast(): exchange(potential(core, local_walkers, own, other, kept, slab, kept_tiles))]
    all_to_all x1 -> x2, starting transfers between devices: 2.92 us -> 9.99 us  [the longest x1 7.33 us: fast(): pieces = exchange(rotated).reshape(-1, 2 * occupied)]
    all_to_all x3 -> x2, blocking collectives: 32 us -> 26.8 us  [the longest x1 14 us: fast(): exchange(add(own, lax.ppermute(sent, 'pair', swap)), axis_index_groups=al...]
    reshape x7 -> x0, local copies, waits for them, and re-layouts: 4.5 us -> none  [the longest x2 2.78 us: per_device(): rotated_piece = shard_piece.reshape(rows_here, occupied, block_rows)]
    ppermute x0 -> x2, waiting for transfers between devices: none -> 3.16 us  [the longest x1 1.63 us: fast(): lax.ppermute(sent, 'pair', swap)]
  transfers between devices with their start and end apart: 1 -> 4, of which waited for: 1 -> 4; matrix products, arithmetic and copies ran while one was open for 0% -> 0% of each run, Pallas kernels for 0% -> 0%
where the time goes in v2:
time: 143 us
  Pallas kernels  55.6 us (39%)
  waiting for transfers between devices  46.2 us (32%)
  blocking collectives  26.8 us (19%)
  starting transfers between devices  10.2 us (7%)
  local copies, waits for them, and re-layouts  3.08 us (2%)
    all_to_all x1, waiting for transfers between devices, fast(): exchange(potential(core, local_walkers, own, other, kept, slab, kept_tiles))  26.8 us
    pallas_call x1, Pallas kernels, bias_partial(): pl.pallas_call(bias_kernel, out_shape=(jax.ShapeDtypeStruct(half_shape, j...  25.1 us
    pallas_call x1, Pallas kernels, potential(): pl.pallas_call(functools.partial(potential_kernel, kept_tiles), out_shape...  25.1 us
    all_to_all x1, waiting for transfers between devices, fast(): pieces = exchange(rotated).reshape(-1, 2 * occupied)  16.2 us
    all_to_all x1, blocking collectives, fast(): exchange(add(own, lax.ppermute(sent, 'pair', swap)), axis_index_groups=al...  14 us
    all_to_all x1, blocking collectives, fast(): own = exchange(copies, axis_index_groups=alike).reshape(-1, lanes)  12.8 us
    all_to_all x1, starting transfers between devices, fast(): pieces = exchange(rotated).reshape(-1, 2 * occupied)  7.33 us
  transfers between devices with their start and end apart: 4, of which 4 were waited for; matrix products, arithmetic and copies ran while one was open for 0% of the time, Pallas kernels for 0%

profile of v2, /device:TPU:0, one launch (start us, length us, event | category | flops | bytes accessed | tf_op | source)
XLA Modules:
  0.0 142.6 jit_solution(2499480104179918928)
XLA Ops:
  0.6 0.0 copy-start.2
  0.6 2.5 %rotate.1 = bf16[32,64,128]{2,1,0:T(8,128)(2,1)} custom-call(f32[2,64,512]{2,1,0:T(8,128)} %walkers_ref.1, f32[2,64,64]{2,1,0:T(8,128)} %inverse_hbm.1), custom_call_target="tpu_custom_call" | custom-call | tf_op jit(solution)/shard_map/rotate/pallas_call | solution.py:58
  3.1 7.3 %all-to-all-start = ((bf16[32,64,128]{2,1,0:T(8,128)(2,1)}), bf16[32,64,128]{2,1,0:T(8,128)(2,1)S(1)}, u32[]{:S(2)}, u32[]{:S(2)}) async-start(bf16[32,64,128]{2,1,0:T(8,128)(2,1)} %rotate.1), calls=%async_computation | async-start | bytes 1048576 | tf_op jit(solution)/shard_map/all_to_all | solution.py:394
  10.5 16.2 %all-to-all-done = bf16[32,64,128]{2,1,0:T(8,128)(2,1)S(1)} async-done(((bf16[32,64,128]{2,1,0:T(8,128)(2,1)}), bf16[32,64,128]{2,1,0:T(8,128)(2,1)S(1)}, u32[]{:S(2)}, u32[]{:S(2)}) %all-to-all-start) | async-done | bytes 524320 | tf_op jit(solution)/shard_map/all_to_all | solution.py:394
  26.7 0.0 copy-start.3
  26.7 0.8 copy-done.3
  27.5 25.1 %bias_partial.1 = (bf16[16,64,128]{2,1,0:T(8,128)(2,1)}, bf16[16,64,128]{2,1,0:T(8,128)(2,1)}, bf16[5632,4096]{1,0:T(8,128)(2,1)S(1)}) custom-call(s32[1]{0:T(128)} %bitcast.core_ref, bf16[2048,128]{1,0:T(8,128)(2,1)} %bitcast.4, bf16[64,128]{1,0:T(8,128)(2,1)} %trial_ref.1, bf16[8192,4096]{1,0:T(8,128)(2,1)} %bitcast.2.slab_ref), custom_call_target="tpu_custom_call" | custom-call | flops 4294967296 | bytes 67108864 | tf_op jit(solution)/shard_map/bias_partial/pallas_call | solution.py:173
  52.6 0.0 copy-start
  52.6 0.2 collective-permute-start
  52.8 1.6 %collective-permute-done.other_ref = bf16[16,64,128]{2,1,0:T(8,128)(2,1)S(1)} collective-permute-done((bf16[16,64,128]{2,1,0:T(8,128)(2,1)}, bf16[16,64,128]{2,1,0:T(8,128)(2,1)S(1)}, u32[]{:S(2)}, u32[]{:S(2)}) %collective-permute-start) | collective-permute-done | bytes 262176 | tf_op jit(solution)/shard_map/ppermute | solution.py:402
  54.5 0.0 copy-start.1
  54.5 0.9 copy-done.1
  55.4 0.1 add.2
  55.5 14.0 %all_to_all.20.in_ref = bf16[16,64,128]{2,1,0:T(8,128)(2,1)S(1)} all-to-all(bf16[16,64,128]{2,1,0:T(8,128)(2,1)S(1)} %add.2), channel_id=1, replica_groups={{0,2,4,6,8,10,12,14,16,18,20,22,24,26,28,30},{1,3,5,7,9,11,13,15,17,19,..., dimensions={0} | all-to-all | bytes 524288 | tf_op jit(solution)/shard_map/all_to_all | solution.py:402
  69.5 0.0 copy-done.2
  69.5 0.1 shift.1
  69.6 12.8 %all_to_all.21 = bf16[16,64,128]{2,1,0:T(8,128)(2,1)S(1)} all-to-all(bf16[16,64,128]{2,1,0:T(8,128)(2,1)S(1)} %get-tuple-element.9), channel_id=1, replica_groups={{0,2,4,6,8,10,12,14,16,18,20,22,24,26,28,30},{1,3,5,7,9,11,13,15,17,19,..., dimensions={0} | all-to-all | bytes 524288 | tf_op jit(solution)/shard_map/all_to_all | solution.py:404
  82.4 0.0 copy-start.4
  82.4 0.0 collective-permute-start.1
  82.4 1.5 %collective-permute-done.1.other_ref = bf16[1024,128]{1,0:T(8,128)(2,1)S(1)} collective-permute-done((bf16[1024,128]{1,0:T(8,128)(2,1)S(1)}, bf16[1024,128]{1,0:T(8,128)(2,1)S(1)}, u32[]{:S(2)}, u32[]{:S(2)}) %collective-permute-start.1) | collective-permute-done | bytes 262176 | tf_op jit(solution)/shard_map/ppermute | solution.py:405
  84.0 0.0 copy-start.5
  84.0 0.0 copy-done.4
  84.0 0.7 copy-done.5
  84.7 25.1 %potential.1 = bf16[32,2,64,128]{3,2,1,0:T(8,128)(2,1)} custom-call(s32[1]{0:T(128)} %bitcast.core_ref, bf16[1024,128]{1,0:T(8,128)(2,1)} %bitcast.6, bf16[1024,128]{1,0:T(8,128)(2,1)} %copy-done.5, bf16[5632,4096]{1,0:T(8,128)(2,1)S(1)} %get-tuple-element.10.kept_ref, bf16[8192,4096]{1,0:T(8,128)(2,1)} %bitcast.2.slab_ref), custom_call_target="tpu_custom_call" | custom-call | flops 4294967296 | bytes 67108864 | tf_op jit(solution)/shard_map/potential/pallas_call | solution.py:311
  109.7 2.7 %all-to-all-start.3 = ((bf16[32,2,64,128]{3,2,1,0:T(8,128)(2,1)}), bf16[32,2,64,128]{3,2,1,0:T(8,128)(2,1)S(1)}, u32[]{:S(2)}, u32[]{:S(2)}) async-start(bf16[32,2,64,128]{3,2,1,0:T(8,128)(2,1)} %potential.1), calls=%async_computation.3 | async-start | bytes 2097152 | tf_op jit(solution)/shard_map/all_to_all | solution.py:406
  112.4 0.6 slice_reduce_fusion
  113.0 26.8 %all-to-all-done.3.refs_0_ = bf16[32,2,64,128]{3,2,1,0:T(8,128)(2,1)S(1)} async-done(((bf16[32,2,64,128]{3,2,1,0:T(8,128)(2,1)}), bf16[32,2,64,128]{3,2,1,0:T(8,128)(2,1)S(1)}, u32[]{:S(2)}, u32[]{:S(2)}) %all-to-all-start.3) | async-done | bytes 1048608 | tf_op jit(solution)/shard_map/all_to_all | solution.py:406
  139.9 0.0 copy-done
  139.9 2.8 %series.1 = f32[2,64,512]{2,1,0:T(8,128)} custom-call(f32[2,64,512]{2,1,0:T(8,128)S(1)} %copy-done, bf16[32,2,64,128]{3,2,1,0:T(8,128)(2,1)S(1)} %all-to-all-done.3.refs_0_), custom_call_target="tpu_custom_call" | custom-call | tf_op jit(solution)/shard_map/series/pallas_call | solution.py:364
Async XLA Ops:
  0.6 68.8 %copy-start.2 = (f32[2,4096]{1,0:T(2,128)S(1)}, f32[2,4096]{1,0:T(2,128)}, u32[]{:S(2)}) copy-start(f32[2,4096]{1,0:T(2,128)} %fields_ref.1) | copy-start | bytes 98308
  3.1 23.6 %all-to-all-start = ((bf16[32,64,128]{2,1,0:T(8,128)(2,1)}), bf16[32,64,128]{2,1,0:T(8,128)(2,1)S(1)}, u32[]{:S(2)}, u32[]{:S(2)}) async-start(bf16[32,64,128]{2,1,0:T(8,128)(2,1)} %rotate.1), calls=%async_computation | async-start | bytes 1048576 | tf_op jit(solution)/shard_map/all_to_all | solution.py:394
  26.7 0.8 copy-start.3
  52.6 87.2 %copy-start = (f32[2,64,512]{2,1,0:T(8,128)S(1)}, f32[2,64,512]{2,1,0:T(8,128)}, u32[]{:S(2)}) copy-start(f32[2,64,512]{2,1,0:T(8,128)} %walkers_ref.1) | copy-start | bytes 786436
  52.6 1.8 %collective-permute-start = (bf16[16,64,128]{2,1,0:T(8,128)(2,1)}, bf16[16,64,128]{2,1,0:T(8,128)(2,1)S(1)}, u32[]{:S(2)}, u32[]{:S(2)}) collective-permute-start(bf16[16,64,128]{2,1,0:T(8,128)(2,1)} %get-tuple-element.8), channel_id=1, source_target_pairs={{0,1},{1,0},{2,3},{3,2},{4,5},{5,4},{6,7},{7,6},{8,9},{9,8},{10,11... | collective-permute-start | bytes 786440 | tf_op jit(solution)/shard_map/ppermute | solution.py:402
  54.5 1.0 copy-start.1
  82.4 1.5 %copy-start.4 = (bf16[16,64,128]{2,1,0:T(8,128)(2,1)}, bf16[16,64,128]{2,1,0:T(8,128)(2,1)S(1)}, u32[]{:S(2)}) copy-start(bf16[16,64,128]{2,1,0:T(8,128)(2,1)S(1)} %all_to_all.21) | copy-start | bytes 786436
  82.4 1.5 %collective-permute-start.1 = (bf16[1024,128]{1,0:T(8,128)(2,1)S(1)}, bf16[1024,128]{1,0:T(8,128)(2,1)S(1)}, u32[]{:S(2)}, u32[]{:S(2)}) collective-permute-start(bf16[1024,128]{1,0:T(8,128)(2,1)S(1)} %bitcast.5), channel_id=1, source_target_pairs={{0,1},{1,0},{2,3},{3,2},{4,5},{5,4},{6,7},{7,6},{8,9},{9,8},{10,11... | collective-permute-start | bytes 786440 | tf_op jit(solution)/shard_map/ppermute | solution.py:405
  84.0 0.7 copy-start.5
  109.7 30.1 %all-to-all-start.3 = ((bf16[32,2,64,128]{3,2,1,0:T(8,128)(2,1)}), bf16[32,2,64,128]{3,2,1,0:T(8,128)(2,1)S(1)}, u32[]{:S(2)}, u32[]{:S(2)}) async-start(bf16[32,2,64,128]{3,2,1,0:T(8,128)(2,1)} %potential.1), calls=%async_computation.3 | async-start | bytes 2097152 | tf_op jit(solution)/shard_map/all_to_all | solution.py:406

commit v3 on v2

--- a/solution.py
+++ b/solution.py
@@ -10,17 +10,21 @@
 time_root = 0.1
 lanes = 128
 tile_rows = 512
-row_group = 16
 ring_slots = 2
-ahead = 3
-stream_slots = 4
+ahead = 6
+period = 4
+early_share = 0.34
 
 mebi = 1 << 20
-grant = 14 * mebi
+grant = 13 * mebi
 highest = lax.Precision.HIGHEST
 whole = pl.BlockSpec(memory_space=pltpu.VMEM)
 anywhere = pl.BlockSpec(memory_space=pltpu.HBM)
 scalar = pl.BlockSpec(memory_space=pltpu.SMEM)
+
+
+def in_vmem(array):
+    return pltpu.with_memory_space_constraint(array, pltpu.VMEM)
 
 
 def in_hbm(array):
@@ -36,7 +40,7 @@
         copy.start()
     for copy in copies:
         copy.wait()
-    count, occupied, orbitals = walkers_ref.shape
+    count, _, orbitals = walkers_ref.shape
     half = out_ref.shape[1] // count
     pairs = orbitals // half // 2
     for w in range(count):
@@ -72,30 +76,61 @@
     )(in_hbm(walkers), in_hbm(inverse))
 
 
-def bias_kernel(core_ref, rotated_ref, trial_ref, slab_ref, own_ref, sent_ref, kept_ref, wide, rows, greens, total, ring, kept_sem, ring_sem):
+def pitch_of(rows):
+    return rows + 8
+
+
+def tile_access(slab_ref, kept_ref, ring, kept_sem, ring_sem):
+    def view(group, i):
+        if i == period - 1:
+            return ring.at[group % ring_slots]
+        start = (group * (period - 1) + i) * tile_rows
+        return kept_ref.at[pl.ds(start, tile_rows)]
+
+    def fetch(group, i):
+        span = pl.ds((group * period + i) * tile_rows, tile_rows)
+        if i == period - 1:
+            sem = ring_sem.at[group % ring_slots]
+        else:
+            sem = kept_sem.at[group * (period - 1) + i]
+        return pltpu.make_async_copy(slab_ref.at[span], view(group, i), sem)
+
+    return fetch, view
+
+
+def load_kernel(early, after_ref, slab_ref, kept_ref, sem):
+    fetch, _ = tile_access(slab_ref, kept_ref, None, sem, None)
+    chosen = [fetch(t // period, t % period) for t in early]
+    for copy in chosen:
+        copy.start()
+    for copy in chosen:
+        copy.wait()
+
+
+def bias_kernel(count, early, core_ref, place_ref, *refs):
+    parts, refs = refs[:count], refs[count:]
+    trial_ref, _, slab_ref, own_ref, sent_ref, kept_ref, wide, rows, greens, total, ring, kept_sem, ring_sem = refs
     vectors = total.shape[1]
     walkers_all = total.shape[0]
-    half = rotated_ref.shape[0] // walkers_all
+    group_walkers = walkers_all // count
+    half = parts[0].shape[0] // group_walkers
     occupied, columns = trial_ref.shape
-    kept_tiles = kept_ref.shape[0] // tile_rows
     tiles = slab_ref.shape[0] // tile_rows
     blocks = vectors // lanes
-
-    def kept_copy(t):
-        span = pl.ds(pl.multiple_of(t * tile_rows, tile_rows), tile_rows)
-        return pltpu.make_async_copy(slab_ref.at[span], kept_ref.at[span], kept_sem.at[t])
-
-    def ring_copy(t):
-        slot = lax.rem(t - kept_tiles, ring_slots)
-        span = pl.ds(pl.multiple_of(t * tile_rows, tile_rows), tile_rows)
-        return pltpu.make_async_copy(slab_ref.at[span], ring.at[slot], ring_sem.at[slot])
-
-    for t in range(min(ahead, kept_tiles)):
-        kept_copy(t).start()
-    wide[: rotated_ref.shape[0], :] = rotated_ref[...].astype(jnp.float32)
+    fetch, view = tile_access(slab_ref, kept_ref, ring, kept_sem, ring_sem)
+
+    for t in range(min(ahead, tiles)):
+        if t not in early:
+            fetch(t // period, t % period).start()
+    pitch = pitch_of(half)
+    for k, part in enumerate(parts):
+        top = (place_ref[0] ^ k) * (group_walkers * pitch)
+        for w in range(group_walkers):
+            row = pl.multiple_of(top + w * pitch, 8)
+            wide[pl.ds(row, half), :] = part[w * half : (w + 1) * half, :].astype(jnp.float32)
     for r in range(half):
         rows[r * walkers_all : (r + 1) * walkers_all, :] = wide[
-            pl.ds(r, walkers_all, stride=half), :
+            pl.ds(r, walkers_all, stride=pitch), :
         ].astype(jnp.bfloat16)
     nothing = jnp.zeros((occupied, columns), jnp.bfloat16)
     trial = trial_ref[...]
@@ -117,41 +152,21 @@
             greens[:, second : second + columns] = piece[:, columns:]
     total[...] = jnp.zeros_like(total)
 
-    @pl.loop(0, kept_tiles)
-    def _(t):
-        start = pl.multiple_of(t * tile_rows, tile_rows)
-        coming = t + ahead
-
-        @pl.when(coming < kept_tiles)
-        def _():
-            kept_copy(coming).start()
-
-        @pl.when((coming >= kept_tiles) & (coming < min(kept_tiles + ring_slots, tiles)))
-        def _():
-            ring_copy(coming).start()
-
-        kept_copy(t).wait()
-        total[...] += jnp.dot(
-            greens[:, pl.ds(start, tile_rows)], kept_ref[pl.ds(start, tile_rows), :],
-            preferred_element_type=jnp.float32,
-        )
-
-    @pl.loop(kept_tiles, tiles)
-    def _(t):
-        start = pl.multiple_of(t * tile_rows, tile_rows)
-        slot = lax.rem(t - kept_tiles, ring_slots)
-        ring_copy(t).wait()
-        total[...] += jnp.dot(
-            greens[:, pl.ds(start, tile_rows)], ring[slot],
-            preferred_element_type=jnp.float32,
-        )
-
-        @pl.when(t + ring_slots < tiles)
-        def _():
-            ring_copy(t + ring_slots).start()
-
+    for group in range(tiles // period):
+        for i in range(period):
+            t = group * period + i
+            if t + ahead < tiles and t + ahead not in early:
+                fetch((t + ahead) // period, (t + ahead) % period).start()
+            if t not in early:
+                fetch(group, i).wait()
+            total[...] += jnp.dot(
+                greens[:, t * tile_rows : (t + 1) * tile_rows], view(group, i)[...],
+                preferred_element_type=jnp.float32,
+            )
+
+    pitch = pitch_of(walkers_all)
     for j in range(blocks):
-        wide[j * walkers_all : (j + 1) * walkers_all, :] = total[:, j * lanes : (j + 1) * lanes]
+        wide[j * pitch : j * pitch + walkers_all, :] = total[:, j * lanes : (j + 1) * lanes]
     local_walkers = own_ref.shape[1] // blocks
     core = core_ref[0]
     for g in range(own_ref.shape[0]):
@@ -159,33 +174,65 @@
             for ref, side in ((own_ref, core), (sent_ref, 1 - core)):
                 row = (2 * g + side) * local_walkers + w
                 ref[g, w * blocks : (w + 1) * blocks, :] = wide[
-                    pl.ds(row, blocks, stride=walkers_all), :
+                    pl.ds(row, blocks, stride=pitch), :
                 ].astype(jnp.bfloat16)
 
 
-def bias_partial(core, local_walkers, rotated, trial, slab, walkers_all, kept_tiles):
+def tiles_of(slab):
+    return slab.shape[0] // tile_rows
+
+
+def early_tiles(slab):
+    kept = [t for t in range(tiles_of(slab)) if t % period < period - 1]
+    return tuple(kept[: int(len(kept) * early_share)])
+
+
+def load(after, slab):
+    vectors = slab.shape[1]
+    kept_tiles = tiles_of(slab) // period * (period - 1)
+    early = early_tiles(slab)
+    return pl.pallas_call(
+        functools.partial(load_kernel, early),
+        out_shape=pltpu.VMEM((kept_tiles * tile_rows, vectors), jnp.bfloat16),
+        in_specs=[pl.BlockSpec(memory_space=pl.ANY), anywhere],
+        out_specs=whole,
+        scratch_shapes=[pltpu.SemaphoreType.DMA((kept_tiles,))],
+        compiler_params=pltpu.CompilerParams(vmem_limit_bytes=grant),
+        cost_estimate=pl.CostEstimate(
+            flops=0,
+            bytes_accessed=2 * len(early) * tile_rows * vectors,
+            transcendentals=0,
+        ),
+        name="load",
+    )(after, slab)
+
+
+def bias_partial(core, place, local_walkers, parts, trial, kept, slab, walkers_all):
     vectors = slab.shape[1]
     pairs = slab.shape[0]
+    count = len(parts)
+    half = parts[0].shape[0] * count // walkers_all
     half_shape = (
         walkers_all // local_walkers // 2, local_walkers * vectors // lanes, lanes
     )
-    height = max(rotated.shape[0], walkers_all * vectors // lanes)
-    return pl.pallas_call(
-        bias_kernel,
+    height = max(walkers_all * pitch_of(half), vectors // lanes * pitch_of(walkers_all))
+    return pl.pallas_call(
+        functools.partial(bias_kernel, count, early_tiles(slab)),
         out_shape=(
             jax.ShapeDtypeStruct(half_shape, jnp.bfloat16),
             jax.ShapeDtypeStruct(half_shape, jnp.bfloat16),
-            pltpu.VMEM((kept_tiles * tile_rows, vectors), jnp.bfloat16),
-        ),
-        in_specs=[scalar, whole, whole, anywhere],
+            pltpu.VMEM(kept.shape, jnp.bfloat16),
+        ),
+        in_specs=[scalar] * 2 + [whole] * (count + 2) + [anywhere],
         out_specs=(whole, whole, whole),
+        input_output_aliases={count + 3: 2},
         scratch_shapes=[
             pltpu.VMEM((height, lanes), jnp.float32),
-            pltpu.VMEM(rotated.shape, jnp.bfloat16),
+            pltpu.VMEM((walkers_all * half, lanes), jnp.bfloat16),
             pltpu.VMEM((walkers_all, pairs), jnp.bfloat16),
             pltpu.VMEM((walkers_all, vectors), jnp.float32),
             pltpu.VMEM((ring_slots, tile_rows, vectors), jnp.bfloat16),
-            pltpu.SemaphoreType.DMA((kept_tiles,)),
+            pltpu.SemaphoreType.DMA((tiles_of(slab),)),
             pltpu.SemaphoreType.DMA((ring_slots,)),
         ],
         compiler_params=pltpu.CompilerParams(vmem_limit_bytes=grant),
@@ -193,7 +240,7 @@
             flops=2 * walkers_all * slab.size, bytes_accessed=2 * slab.size, transcendentals=0
         ),
         name="bias_partial",
-    )(core, rotated, trial, slab)
+    )(core, place, *[in_vmem(part) for part in parts], trial, pltpu.with_memory_space_constraint(kept, pltpu.VMEM), slab)
 
 
 def add_kernel(own_ref, other_ref, out_ref):
@@ -213,7 +260,7 @@
 
 
 def shift_kernel(in_ref, fields_ref, copies_ref, log_ref, turned):
-    count, rows, _ = in_ref.shape
+    count, _, _ = in_ref.shape
     local_walkers, vectors = fields_ref.shape
     blocks = vectors // lanes
     added = in_ref[0].astype(jnp.float32)
@@ -254,71 +301,69 @@
     )(incoming, fields)
 
 
-def potential_kernel(kept_tiles, core_ref, own_ref, other_ref, kept_ref, slab_ref, out_ref, wide, shifted, product, ring, ring_sem):
+def potential_kernel(core_ref, own_ref, other_ref, kept_ref, slab_ref, out_ref, wide, shifted, product, ring, ring_sem):
     half_rows = own_ref.shape[0]
     walkers_all, vectors = shifted.shape
     local_walkers = walkers_all // out_ref.shape[0]
     blocks = vectors // lanes
-    tiles = slab_ref.shape[0] // tile_rows
+    groups = slab_ref.shape[0] // tile_rows // period
     per_tile = tile_rows // lanes
-    group = row_group // per_tile
+    group_rows = period * per_tile
     core = core_ref[0]
-
-    def ring_copy(t):
-        slot = (t - kept_tiles) % ring_slots
-        span = pl.ds(t * tile_rows, tile_rows)
-        return pltpu.make_async_copy(slab_ref.at[span], ring.at[slot], ring_sem.at[slot])
-
-    for t in range(kept_tiles, min(kept_tiles + ring_slots, tiles)):
-        ring_copy(t).start()
-    wide[:half_rows, :] = own_ref[...].astype(jnp.float32)
-    wide[half_rows:, :] = other_ref[...].astype(jnp.float32)
+    fetch, view = tile_access(slab_ref, kept_ref, ring, None, ring_sem)
+
+    for group in range(min(ring_slots, groups)):
+        fetch(group, period - 1).start()
+    pitch = pitch_of(blocks)
+    for m in range(walkers_all):
+        ref, row = (own_ref, m * blocks) if m * blocks < half_rows else (
+            other_ref, m * blocks - half_rows
+        )
+        wide[m * pitch : m * pitch + blocks, :] = ref[row : row + blocks, :].astype(jnp.float32)
     for j in range(blocks):
         shifted[:, j * lanes : (j + 1) * lanes] = wide[
-            pl.ds(j, walkers_all, stride=blocks), :
+            pl.ds(j, walkers_all, stride=pitch), :
         ].astype(jnp.bfloat16)
-    for t in range(tiles):
-        if t < kept_tiles:
-            tile = kept_ref[t * tile_rows : (t + 1) * tile_rows, :]
-        else:
-            ring_copy(t).wait()
-            tile = ring[(t - kept_tiles) % ring_slots]
-        values = lax.dot_general(
-            shifted[...], tile, (((1,), (1,)), ((), ())), preferred_element_type=jnp.float32
-        )
-        if t >= kept_tiles and t + ring_slots < tiles:
-            ring_copy(t + ring_slots).start()
-        place = t % group * per_tile
-        for r in range(per_tile):
-            product[(place + r) * walkers_all : (place + r + 1) * walkers_all, :] = values[
-                :, r * lanes : (r + 1) * lanes
-            ]
-        if t % group == group - 1:
-            base = t // group * row_group
-            for m in range(walkers_all):
-                side, rest = divmod(m, walkers_all // 2)
-                g, w = divmod(rest, local_walkers)
-                owner = 2 * g + (core if side == 0 else 1 - core)
-                out_ref[owner, w, base : base + row_group, :] = product[
-                    pl.ds(m, row_group, stride=walkers_all), :
-                ].astype(jnp.bfloat16)
-
-
-def potential(core, local_walkers, own, other, kept, slab, kept_tiles):
+    pitch = pitch_of(walkers_all)
+    for group in range(groups):
+        half = group % 2
+        for i in range(period):
+            if i == period - 1:
+                fetch(group, i).wait()
+            values = lax.dot_general(
+                view(group, i)[...], shifted[...], (((1,), (1,)), ((), ())),
+                preferred_element_type=jnp.float32,
+            ).T
+            for r in range(per_tile):
+                row = (i * per_tile + r) * pitch
+                product[half, row : row + walkers_all, :] = values[:, r * lanes : (r + 1) * lanes]
+        if group + ring_slots < groups:
+            fetch(group + ring_slots, period - 1).start()
+        base = group * group_rows
+        for m in range(walkers_all):
+            side, rest = divmod(m, walkers_all // 2)
+            g, w = divmod(rest, local_walkers)
+            owner = 2 * g + (core if side == 0 else 1 - core)
+            out_ref[owner, w, base : base + group_rows, :] = product[
+                half, pl.ds(m, group_rows, stride=pitch), :
+            ].astype(jnp.bfloat16)
+
+
+def potential(core, local_walkers, own, other, kept, slab):
     vectors = slab.shape[1]
     walkers_all = 2 * own.shape[0] * lanes // vectors
     rows = slab.shape[0] // lanes
     return pl.pallas_call(
-        functools.partial(potential_kernel, kept_tiles),
+        potential_kernel,
         out_shape=jax.ShapeDtypeStruct(
             (walkers_all // local_walkers, local_walkers, rows, lanes), jnp.bfloat16
         ),
         in_specs=[scalar, whole, whole, whole, anywhere],
         out_specs=whole,
         scratch_shapes=[
-            pltpu.VMEM((2 * own.shape[0], lanes), jnp.float32),
+            pltpu.VMEM((walkers_all * pitch_of(vectors // lanes), lanes), jnp.float32),
             pltpu.VMEM((walkers_all, vectors), jnp.bfloat16),
-            pltpu.VMEM((row_group * walkers_all, lanes), jnp.float32),
+            pltpu.VMEM((2, tile_rows // lanes * period * pitch_of(walkers_all), lanes), jnp.float32),
             pltpu.VMEM((ring_slots, tile_rows, vectors), jnp.bfloat16),
             pltpu.SemaphoreType.DMA((ring_slots,)),
         ],
@@ -332,7 +377,7 @@
 
 def series_kernel(walk_count, walkers_ref, *refs):
     pieces, out_ref, matrix = refs[:-2], refs[-2], refs[-1]
-    local_walkers, occupied, orbitals = walkers_ref.shape
+    local_walkers, _, orbitals = walkers_ref.shape
     pair_count = pieces[0].shape[0] // walk_count
     block_rows = orbitals // pair_count
     for w in range(local_walkers):
@@ -360,7 +405,7 @@
 
 
 def series(walkers, pieces, walk_count):
-    local_walkers, occupied, orbitals = walkers.shape
+    local_walkers, _, orbitals = walkers.shape
     return pl.pallas_call(
         functools.partial(series_kernel, walk_count),
         out_shape=jax.ShapeDtypeStruct(walkers.shape, jnp.float32),
@@ -372,38 +417,38 @@
     )(walkers, *pieces)
 
 
-kept_share = 0.6875
-
-
 def fast(walkers, inverse_intersection, trial, fields, cholesky):
     pair_count = lax.axis_size("pair")
     walk_count = lax.axis_size("walk")
     device_count = walk_count * pair_count
-    local_walkers, occupied, orbitals = walkers.shape
+    local_walkers, occupied, _ = walkers.shape
     walkers_all = local_walkers * device_count
     vectors = cholesky.shape[2]
-    blocks = vectors // lanes
     slab = cholesky.reshape(-1, vectors)
-    tiles = slab.shape[0] // tile_rows
-    kept_tiles = int(tiles * kept_share)
     everyone = ("walk", "pair")
     exchange = functools.partial(
         lax.all_to_all, axis_name=everyone, split_axis=0, concat_axis=0, tiled=True
     )
-    rotated = rotate(walkers, inverse_intersection, walk_count, pair_count)
-    pieces = exchange(rotated).reshape(-1, 2 * occupied)
-    place = lax.axis_index("pair")
-    core = lax.rem(place, 2).reshape(1)
+    rotated = rotate(walkers, inverse_intersection, 1, pair_count)
+    regrouped = lax.all_to_all(rotated, "pair", split_axis=0, concat_axis=0, tiled=True)
+    regrouped = regrouped.reshape(-1, 2 * occupied)
+    parts = [regrouped]
+    for k in range(1, walk_count):
+        route = [(i, i ^ k) for i in range(walk_count)]
+        parts.append(lax.ppermute(regrouped, "walk", route))
+    kept = load(regrouped, slab)
+    core = lax.rem(lax.axis_index("pair"), 2).reshape(1)
+    place = lax.axis_index("walk").reshape(1)
     swap = [(i, i ^ 1) for i in range(pair_count)]
     alike = [list(range(c, device_count, 2)) for c in range(2)]
     own, sent, kept = bias_partial(
-        core, local_walkers, pieces, trial, slab, walkers_all, kept_tiles
+        core, place, local_walkers, parts, trial, kept, slab, walkers_all
     )
     incoming = exchange(add(own, lax.ppermute(sent, "pair", swap)), axis_index_groups=alike)
     copies, log_rows = shift(incoming, fields)
     own = exchange(copies, axis_index_groups=alike).reshape(-1, lanes)
     other = lax.ppermute(own, "pair", swap)
-    arrived = [exchange(potential(core, local_walkers, own, other, kept, slab, kept_tiles))]
+    arrived = [exchange(potential(core, local_walkers, own, other, kept, slab))]
     return (series(walkers, arrived, walk_count), log_rows[:, 0])
 
 
@@ -457,6 +502,7 @@
         summed = summed + series_term
     return (summed, log_importance)
 
+
 def per_device(walkers, inverse_intersection, trial, fields, cholesky):
     block_rows, block_cols, vectors = cholesky.shape
     fits = (
@@ -464,7 +510,9 @@
         and vectors % lanes == 0
         and 2 * walkers.shape[1] == lanes
         and block_rows % 32 == 0
+        and block_rows * block_cols % (period * tile_rows) == 0
         and lax.axis_size("pair") % 2 == 0
+        and lax.axis_size("walk") & (lax.axis_size("walk") - 1) == 0
     )
     step = fast if fits else plain
     return step(walkers, inverse_intersection, trial, fields, cholesky)

time: 143 us -> 134 us (0.937)
  waiting for transfers between devices: 46.2 us -> 30.1 us
  blocking collectives: 26.8 us -> 41.1 us
  starting transfers between devices: 10.2 us -> 6.22 us
  Pallas kernels: 55.6 us -> 51.7 us
    all_to_all x2 -> x1, waiting for transfers between devices: 43.1 us -> 26.8 us  [fast(): arrived = [exchange(potential(core, local_walkers, own, other, kept, slab))]]
    all_to_all x0 -> x1, blocking collectives: none -> 12.9 us  [fast(): lax.all_to_all(rotated, 'pair', split_axis=0, concat_axis=0, tiled=True)]
    all_to_all x2 -> x1, starting transfers between devices: 9.99 us -> 2.66 us  [fast(): arrived = [exchange(potential(core, local_walkers, own, other, kept, slab))]]
    ppermute x0 -> x3, starting transfers between devices: none -> 3.49 us  [fast(): parts.append(lax.ppermute(regrouped, 'walk', route))]
    pallas_call x2 -> x3, Pallas kernels: 50.2 us -> 47 us  [the longest x1 22.8 us: potential(): pl.pallas_call(potential_kernel, out_shape=jax.ShapeDtypeStruct((walkers_...]
  transfers between devices with their start and end apart: 4 -> 6, of which waited for: 4 -> 3; matrix products, arithmetic and copies ran while one was open for 0% -> 0% of each run, Pallas kernels for 0% -> 4%
where the time goes in v3:
time: 134 us; the launch traced here: 133 us
  Pallas kernels  51.7 us (39%)
  blocking collectives  41.1 us (31%)
  waiting for transfers between devices  30.1 us (22%)
  starting transfers between devices  6.22 us (5%)
  local copies, waits for them, and re-layouts  3.2 us (2%)
    all_to_all x1, waiting for transfers between devices, fast(): arrived = [exchange(potential(core, local_walkers, own, other, kept, slab))]  26.8 us
    pallas_call x1, Pallas kernels, potential(): pl.pallas_call(potential_kernel, out_shape=jax.ShapeDtypeStruct((walkers_...  22.8 us
    pallas_call x1, Pallas kernels, bias_partial(): pl.pallas_call(functools.partial(bias_kernel, count, early_tiles(slab)),...  18.3 us
    all_to_all x1, blocking collectives, fast(): exchange(add(own, lax.ppermute(sent, 'pair', swap)), axis_index_groups=al...  15.4 us
    all_to_all x1, blocking collectives, fast(): lax.all_to_all(rotated, 'pair', split_axis=0, concat_axis=0, tiled=True)  12.9 us
    all_to_all x1, blocking collectives, fast(): own = exchange(copies, axis_index_groups=alike).reshape(-1, lanes)  12.8 us
    pallas_call x1, Pallas kernels, load(): pl.pallas_call(functools.partial(load_kernel, early), out_shape=pltpu.VME...  5.96 us
    ppermute x3, starting transfers between devices, fast(): parts.append(lax.ppermute(regrouped, 'walk', route))  3.49 us
  transfers between devices with their start and end apart: 6, of which 3 were waited for; matrix products, arithmetic and copies ran while one was open for 0% of the time, Pallas kernels for 4%

profile of v3, /device:TPU:0, one launch (start us, length us, event | category | flops | bytes accessed | tf_op | source)
XLA Modules:
  0.0 133.1 jit_solution(17026241294953470456)
XLA Ops:
  0.6 1.7 %rotate.1 = bf16[8,64,128]{2,1,0:T(8,128)(2,1)S(1)} custom-call(f32[2,64,512]{2,1,0:T(8,128)} %walkers_ref.1, f32[2,64,64]{2,1,0:T(8,128)} %inverse_hbm.1), custom_call_target="tpu_custom_call" | custom-call | tf_op jit(solution)/shard_map/rotate/pallas_call | solution.py:62
  2.3 12.9 %all_to_all.20 = bf16[8,64,128]{2,1,0:T(8,128)(2,1)S(1)} all-to-all(bf16[8,64,128]{2,1,0:T(8,128)(2,1)S(1)} %rotate.1), channel_id=1, replica_groups=mesh['walk'=4,'pair'=8] {'pair'}, dimensions={0} | all-to-all | bytes 262144 | tf_op jit(solution)/shard_map/all_to_all | solution.py:433
  15.2 0.0 copy-start
  15.2 2.4 %collective-permute-start.2 = (bf16[512,128]{1,0:T(8,128)(2,1)S(1)}, bf16[512,128]{1,0:T(8,128)(2,1)S(1)}, u32[]{:S(2)}, u32[]{:S(2)}) collective-permute-start(bf16[512,128]{1,0:T(8,128)(2,1)S(1)} %bitcast.5), channel_id=1, source_target_pairs={{0,24},{8,16},{16,8},{24,0},{1,25},{9,17},{17,9},{25,1},{2,26},{10... | collective-permute-start | bytes 393224 | tf_op jit(solution)/shard_map/ppermute | solution.py:438
  17.7 0.5 collective-permute-start.1
  18.2 0.5 collective-permute-start
  18.7 0.0 copy-done
  18.7 6.0 %load.1.refs_5_ = bf16[6144,4096]{1,0:T(8,128)(2,1)S(1)} custom-call(bf16[512,128]{1,0:T(8,128)(2,1)} %bitcast.8, bf16[8192,4096]{1,0:T(8,128)(2,1)} %bitcast.3.slab_ref.refs_6_), custom_call_target="tpu_custom_call" | custom-call | bytes 16777216 | tf_op jit(solution)/shard_map/load/pallas_call | solution.py:194
  24.7 0.0 collective-permute-done.2.refs_3_
  24.7 0.0 collective-permute-done.1.refs_2_
  24.7 0.0 collective-permute-done.refs_1_
  24.7 0.0 copy-start.1
  24.8 0.9 copy-done.1
  25.6 0.0 copy-start.4
  25.7 18.3 %bias_partial.1 = (bf16[16,64,128]{2,1,0:T(8,128)(2,1)}, bf16[16,64,128]{2,1,0:T(8,128)(2,1)}, bf16[6144,4096]{1,0:T(8,128)(2,1)S(1)}) custom-call(s32[1]{0:T(128)} %bitcast.core_ref, s32[1]{0:T(128)} %bitcast.1.place_ref, bf16[512,128]{1,0:T(8,128)(2,1)S(1)} %bitcast.9, ...), custom_call_target="tpu_custom_call", output_to_operand_aliasing={{2}: (7, {})} | custom-call | flops 4294967296 | bytes 67108864 | tf_op jit(solution)/shard_map/bias_partial/pallas_call | solution.py:219
  43.9 0.1 collective-permute-start.3
  44.0 1.7 %collective-permute-done.3.other_ref = bf16[16,64,128]{2,1,0:T(8,128)(2,1)S(1)} collective-permute-done((bf16[16,64,128]{2,1,0:T(8,128)(2,1)}, bf16[16,64,128]{2,1,0:T(8,128)(2,1)S(1)}, u32[]{:S(2)}, u32[]{:S(2)}) %collective-permute-start.3) | collective-permute-done | bytes 262176 | tf_op jit(solution)/shard_map/ppermute | solution.py:447
  45.7 0.0 copy-start.3
  45.7 0.9 copy-done.3
  46.7 0.1 add.2
  46.8 15.4 %all_to_all.21.in_ref = bf16[16,64,128]{2,1,0:T(8,128)(2,1)S(1)} all-to-all(bf16[16,64,128]{2,1,0:T(8,128)(2,1)S(1)} %add.2), channel_id=1, replica_groups={{0,2,4,6,8,10,12,14,16,18,20,22,24,26,28,30},{1,3,5,7,9,11,13,15,17,19,..., dimensions={0} | all-to-all | bytes 524288 | tf_op jit(solution)/shard_map/all_to_all | solution.py:447
  62.1 0.0 copy-done.4
  62.1 0.1 shift.1
  62.3 12.8 %all_to_all.22 = bf16[16,64,128]{2,1,0:T(8,128)(2,1)S(1)} all-to-all(bf16[16,64,128]{2,1,0:T(8,128)(2,1)S(1)} %get-tuple-element.9), channel_id=1, replica_groups={{0,2,4,6,8,10,12,14,16,18,20,22,24,26,28,30},{1,3,5,7,9,11,13,15,17,19,..., dimensions={0} | all-to-all | bytes 524288 | tf_op jit(solution)/shard_map/all_to_all | solution.py:449
  75.1 0.0 copy-start.5
  75.1 0.0 collective-permute-start.4
  75.1 1.5 %collective-permute-done.4.other_ref = bf16[1024,128]{1,0:T(8,128)(2,1)S(1)} collective-permute-done((bf16[1024,128]{1,0:T(8,128)(2,1)S(1)}, bf16[1024,128]{1,0:T(8,128)(2,1)S(1)}, u32[]{:S(2)}, u32[]{:S(2)}) %collective-permute-start.4) | collective-permute-done | bytes 262176 | tf_op jit(solution)/shard_map/ppermute | solution.py:450
  76.6 0.0 copy-start.6
  76.7 0.0 copy-done.5
  76.7 0.7 copy-done.6
  77.4 0.0 copy-start.2
  77.4 22.8 %potential.1 = bf16[32,2,64,128]{3,2,1,0:T(8,128)(2,1)} custom-call(s32[1]{0:T(128)} %bitcast.core_ref, bf16[1024,128]{1,0:T(8,128)(2,1)} %bitcast.11, bf16[1024,128]{1,0:T(8,128)(2,1)} %copy-done.6, bf16[6144,4096]{1,0:T(8,128)(2,1)S(1)} %get-tuple-element.10.kept_ref, bf16[8192,4096]{1,0:T(8,128)(2,1)} %bitcast.3.slab_ref.refs_6_), custom_call_target="tpu_custom_call" | custom-call | flops 4294967296 | bytes 67108864 | tf_op jit(solution)/shard_map/potential/pallas_call | solution.py:356
  100.2 2.7 %all-to-all-start.3 = ((bf16[32,2,64,128]{3,2,1,0:T(8,128)(2,1)}), bf16[32,2,64,128]{3,2,1,0:T(8,128)(2,1)S(1)}, u32[]{:S(2)}, u32[]{:S(2)}) async-start(bf16[32,2,64,128]{3,2,1,0:T(8,128)(2,1)} %potential.1), calls=%async_computation.3 | async-start | bytes 2097152 | tf_op jit(solution)/shard_map/all_to_all | solution.py:451
  102.8 0.6 slice_reduce_fusion
  103.5 26.8 %all-to-all-done.3.refs_0_ = bf16[32,2,64,128]{3,2,1,0:T(8,128)(2,1)S(1)} async-done(((bf16[32,2,64,128]{3,2,1,0:T(8,128)(2,1)}), bf16[32,2,64,128]{3,2,1,0:T(8,128)(2,1)S(1)}, u32[]{:S(2)}, u32[]{:S(2)}) %all-to-all-start.3) | async-done | bytes 1048608 | tf_op jit(solution)/shard_map/all_to_all | solution.py:451
  130.3 0.0 copy-done.2
  130.3 2.8 %series.1 = f32[2,64,512]{2,1,0:T(8,128)} custom-call(f32[2,64,512]{2,1,0:T(8,128)S(1)} %copy-done.2, bf16[32,2,64,128]{3,2,1,0:T(8,128)(2,1)S(1)} %all-to-all-done.3.refs_0_), custom_call_target="tpu_custom_call" | custom-call | tf_op jit(solution)/shard_map/series/pallas_call | solution.py:409
Async XLA Ops:
  15.2 3.5 %copy-start = (bf16[8,64,128]{2,1,0:T(8,128)(2,1)}, bf16[8,64,128]{2,1,0:T(8,128)(2,1)S(1)}, u32[]{:S(2)}) copy-start(bf16[8,64,128]{2,1,0:T(8,128)(2,1)S(1)} %all_to_all.20) | copy-start | bytes 393220
  15.2 9.5 %collective-permute-start.2 = (bf16[512,128]{1,0:T(8,128)(2,1)S(1)}, bf16[512,128]{1,0:T(8,128)(2,1)S(1)}, u32[]{:S(2)}, u32[]{:S(2)}) collective-permute-start(bf16[512,128]{1,0:T(8,128)(2,1)S(1)} %bitcast.5), channel_id=1, source_target_pairs={{0,24},{8,16},{16,8},{24,0},{1,25},{9,17},{17,9},{25,1},{2,26},{10... | collective-permute-start | bytes 393224 | tf_op jit(solution)/shard_map/ppermute | solution.py:438
  17.7 7.0 %collective-permute-start.1 = (bf16[512,128]{1,0:T(8,128)(2,1)S(1)}, bf16[512,128]{1,0:T(8,128)(2,1)S(1)}, u32[]{:S(2)}, u32[]{:S(2)}) collective-permute-start(bf16[512,128]{1,0:T(8,128)(2,1)S(1)} %bitcast.6), channel_id=1, source_target_pairs={{0,16},{8,24},{16,0},{24,8},{1,17},{9,25},{17,1},{25,9},{2,18},{10... | collective-permute-start | bytes 393224 | tf_op jit(solution)/shard_map/ppermute | solution.py:438
  18.2 6.5 %collective-permute-start = (bf16[512,128]{1,0:T(8,128)(2,1)S(1)}, bf16[512,128]{1,0:T(8,128)(2,1)S(1)}, u32[]{:S(2)}, u32[]{:S(2)}) collective-permute-start(bf16[512,128]{1,0:T(8,128)(2,1)S(1)} %bitcast.7), channel_id=1, source_target_pairs={{0,8},{8,0},{16,24},{24,16},{1,9},{9,1},{17,25},{25,17},{2,10},{10... | collective-permute-start | bytes 393224 | tf_op jit(solution)/shard_map/ppermute | solution.py:438
  24.7 0.9 copy-start.1
  25.6 36.5 %copy-start.4 = (f32[2,4096]{1,0:T(2,128)S(1)}, f32[2,4096]{1,0:T(2,128)}, u32[]{:S(2)}) copy-start(f32[2,4096]{1,0:T(2,128)} %fields_ref.1) | copy-start | bytes 98308
  43.9 1.8 %collective-permute-start.3 = (bf16[16,64,128]{2,1,0:T(8,128)(2,1)}, bf16[16,64,128]{2,1,0:T(8,128)(2,1)S(1)}, u32[]{:S(2)}, u32[]{:S(2)}) collective-permute-start(bf16[16,64,128]{2,1,0:T(8,128)(2,1)} %get-tuple-element.8), channel_id=1, source_target_pairs={{0,1},{1,0},{2,3},{3,2},{4,5},{5,4},{6,7},{7,6},{8,9},{9,8},{10,11... | collective-permute-start | bytes 786440 | tf_op jit(solution)/shard_map/ppermute | solution.py:447
  45.7 1.0 copy-start.3
  75.1 1.5 %copy-start.5 = (bf16[16,64,128]{2,1,0:T(8,128)(2,1)}, bf16[16,64,128]{2,1,0:T(8,128)(2,1)S(1)}, u32[]{:S(2)}) copy-start(bf16[16,64,128]{2,1,0:T(8,128)(2,1)S(1)} %all_to_all.22) | copy-start | bytes 786436
  75.1 1.5 %collective-permute-start.4 = (bf16[1024,128]{1,0:T(8,128)(2,1)S(1)}, bf16[1024,128]{1,0:T(8,128)(2,1)S(1)}, u32[]{:S(2)}, u32[]{:S(2)}) collective-permute-start(bf16[1024,128]{1,0:T(8,128)(2,1)S(1)} %bitcast.10), channel_id=1, source_target_pairs={{0,1},{1,0},{2,3},{3,2},{4,5},{5,4},{6,7},{7,6},{8,9},{9,8},{10,11... | collective-permute-start | bytes 786440 | tf_op jit(solution)/shard_map/ppermute | solution.py:450
  76.6 0.7 copy-start.6
  77.4 52.9 %copy-start.2 = (f32[2,64,512]{2,1,0:T(8,128)S(1)}, f32[2,64,512]{2,1,0:T(8,128)}, u32[]{:S(2)}) copy-start(f32[2,64,512]{2,1,0:T(8,128)} %walkers_ref.1) | copy-start | bytes 786436
  100.2 30.1 %all-to-all-start.3 = ((bf16[32,2,64,128]{3,2,1,0:T(8,128)(2,1)}), bf16[32,2,64,128]{3,2,1,0:T(8,128)(2,1)S(1)}, u32[]{:S(2)}, u32[]{:S(2)}) async-start(bf16[32,2,64,128]{3,2,1,0:T(8,128)(2,1)} %potential.1), calls=%async_computation.3 | async-start | bytes 2097152 | tf_op jit(solution)/shard_map/all_to_all | solution.py:451

commit v4 on v3

--- a/solution.py
+++ b/solution.py
@@ -150,8 +150,6 @@
             second = (half + r0 + r) * columns
             greens[:, first : first + columns] = piece[:, :columns]
             greens[:, second : second + columns] = piece[:, columns:]
-    total[...] = jnp.zeros_like(total)
-
     for group in range(tiles // period):
         for i in range(period):
             t = group * period + i
@@ -159,10 +157,11 @@
                 fetch((t + ahead) // period, (t + ahead) % period).start()
             if t not in early:
                 fetch(group, i).wait()
-            total[...] += jnp.dot(
+            product = jnp.dot(
                 greens[:, t * tile_rows : (t + 1) * tile_rows], view(group, i)[...],
                 preferred_element_type=jnp.float32,
             )
+            total[...] = product if t == 0 else total[...] + product
 
     pitch = pitch_of(walkers_all)
     for j in range(blocks):
@@ -194,7 +193,7 @@
     return pl.pallas_call(
         functools.partial(load_kernel, early),
         out_shape=pltpu.VMEM((kept_tiles * tile_rows, vectors), jnp.bfloat16),
-        in_specs=[pl.BlockSpec(memory_space=pl.ANY), anywhere],
+        in_specs=[whole, anywhere],
         out_specs=whole,
         scratch_shapes=[pltpu.SemaphoreType.DMA((kept_tiles,))],
         compiler_params=pltpu.CompilerParams(vmem_limit_bytes=grant),
@@ -204,7 +203,7 @@
             transcendentals=0,
         ),
         name="load",
-    )(after, slab)
+    )(in_vmem(after), slab)
 
 
 def bias_partial(core, place, local_walkers, parts, trial, kept, slab, walkers_all):
@@ -219,7 +218,7 @@
     return pl.pallas_call(
         functools.partial(bias_kernel, count, early_tiles(slab)),
         out_shape=(
-            jax.ShapeDtypeStruct(half_shape, jnp.bfloat16),
+            pltpu.VMEM(half_shape, jnp.bfloat16),
             jax.ShapeDtypeStruct(half_shape, jnp.bfloat16),
             pltpu.VMEM(kept.shape, jnp.bfloat16),
         ),
@@ -256,7 +255,7 @@
         out_specs=whole,
         compiler_params=pltpu.CompilerParams(vmem_limit_bytes=4 * mebi),
         name="add",
-    )(own, other)
+    )(in_vmem(own), other)
 
 
 def shift_kernel(in_ref, fields_ref, copies_ref, log_ref, turned):

time: 134 us -> 132 us (0.985)
  local copies, waits for them, and re-layouts: 3.2 us -> 1.34 us
    unnamed x14 -> x8, local copies, waits for them, and re-layouts: 2.58 us -> 0.72 us
  transfers between devices with their start and end apart: 6 -> 6, of which waited for: 3 -> 3; matrix products, arithmetic and copies ran while one was open for 0% -> 0% of each run, Pallas kernels for 4% -> 5%
where the time goes in v4:
time: 132 us; the launch traced here: 131 us
  Pallas kernels  51.7 us (39%)
  blocking collectives  41.1 us (31%)
  waiting for transfers between devices  30.1 us (23%)
  starting transfers between devices  6.22 us (5%)
  local copies, waits for them, and re-layouts  1.34 us (1%)
    all_to_all x1, waiting for transfers between devices, fast(): arrived = [exchange(potential(core, local_walkers, own, other, kept, slab))]  26.8 us
    pallas_call x1, Pallas kernels, potential(): pl.pallas_call(potential_kernel, out_shape=jax.ShapeDtypeStruct((walkers_...  22.8 us
    pallas_call x1, Pallas kernels, bias_partial(): pl.pallas_call(functools.partial(bias_kernel, count, early_tiles(slab)),...  18.3 us
    all_to_all x1, blocking collectives, fast(): exchange(add(own, lax.ppermute(sent, 'pair', swap)), axis_index_groups=al...  15.4 us
    all_to_all x1, blocking collectives, fast(): lax.all_to_all(rotated, 'pair', split_axis=0, concat_axis=0, tiled=True)  12.9 us
    all_to_all x1, blocking collectives, fast(): own = exchange(copies, axis_index_groups=alike).reshape(-1, lanes)  12.8 us
    pallas_call x1, Pallas kernels, load(): pl.pallas_call(functools.partial(load_kernel, early), out_shape=pltpu.VME...  5.96 us
    ppermute x3, starting transfers between devices, fast(): parts.append(lax.ppermute(regrouped, 'walk', route))  3.49 us
  transfers between devices with their start and end apart: 6, of which 3 were waited for; matrix products, arithmetic and copies ran while one was open for 0% of the time, Pallas kernels for 5%

profile of v4, /device:TPU:0, one launch (start us, length us, event | category | flops | bytes accessed | tf_op | source)
XLA Modules:
  0.0 131.2 jit_solution(14265202966203190731)
XLA Ops:
  0.6 1.7 %rotate.1 = bf16[8,64,128]{2,1,0:T(8,128)(2,1)S(1)} custom-call(f32[2,64,512]{2,1,0:T(8,128)} %walkers_ref.1, f32[2,64,64]{2,1,0:T(8,128)} %inverse_hbm.1), custom_call_target="tpu_custom_call" | custom-call | tf_op jit(solution)/shard_map/rotate/pallas_call | solution.py:62
  2.3 12.9 %all_to_all.20 = bf16[8,64,128]{2,1,0:T(8,128)(2,1)S(1)} all-to-all(bf16[8,64,128]{2,1,0:T(8,128)(2,1)S(1)} %rotate.1), channel_id=1, replica_groups=mesh['walk'=4,'pair'=8] {'pair'}, dimensions={0} | all-to-all | bytes 262144 | tf_op jit(solution)/shard_map/all_to_all | solution.py:432
  15.2 2.4 %collective-permute-start.2 = (bf16[512,128]{1,0:T(8,128)(2,1)S(1)}, bf16[512,128]{1,0:T(8,128)(2,1)S(1)}, u32[]{:S(2)}, u32[]{:S(2)}) collective-permute-start(bf16[512,128]{1,0:T(8,128)(2,1)S(1)} %bitcast.5), channel_id=1, source_target_pairs={{0,24},{8,16},{16,8},{24,0},{1,25},{9,17},{17,9},{25,1},{2,26},{10... | collective-permute-start | bytes 393224 | tf_op jit(solution)/shard_map/ppermute | solution.py:437
  17.7 0.5 collective-permute-start.1
  18.2 0.5 collective-permute-start
  18.7 6.0 %load.1.refs_5_ = bf16[6144,4096]{1,0:T(8,128)(2,1)S(1)} custom-call(bf16[512,128]{1,0:T(8,128)(2,1)S(1)} %bitcast.8, bf16[8192,4096]{1,0:T(8,128)(2,1)} %bitcast.3.slab_ref.refs_6_), custom_call_target="tpu_custom_call" | custom-call | bytes 16777216 | tf_op jit(solution)/shard_map/load/pallas_call | solution.py:193
  24.7 0.0 collective-permute-done.2.refs_3_
  24.7 0.0 collective-permute-done.1.refs_2_
  24.7 0.0 collective-permute-done.refs_1_
  24.7 0.0 copy-start.1
  24.7 18.3 %bias_partial.1 = (bf16[16,64,128]{2,1,0:T(8,128)(2,1)S(1)}, bf16[16,64,128]{2,1,0:T(8,128)(2,1)}, bf16[6144,4096]{1,0:T(8,128)(2,1)S(1)}) custom-call(s32[1]{0:T(128)} %bitcast.core_ref, s32[1]{0:T(128)} %bitcast.1.place_ref, bf16[512,128]{1,0:T(8,128)(2,1)S(1)} %bitcast.9, ...), custom_call_target="tpu_custom_call", output_to_operand_aliasing={{2}: (7, {})} | custom-call | flops 4294967296 | bytes 67108864 | tf_op jit(solution)/shard_map/bias_partial/pallas_call | solution.py:218
  43.0 0.1 collective-permute-start.3
  43.1 1.7 %collective-permute-done.3.other_ref = bf16[16,64,128]{2,1,0:T(8,128)(2,1)S(1)} collective-permute-done((bf16[16,64,128]{2,1,0:T(8,128)(2,1)}, bf16[16,64,128]{2,1,0:T(8,128)(2,1)S(1)}, u32[]{:S(2)}, u32[]{:S(2)}) %collective-permute-start.3) | collective-permute-done | bytes 262176 | tf_op jit(solution)/shard_map/ppermute | solution.py:446
  44.8 0.1 add.2
  44.9 15.4 %all_to_all.21.in_ref = bf16[16,64,128]{2,1,0:T(8,128)(2,1)S(1)} all-to-all(bf16[16,64,128]{2,1,0:T(8,128)(2,1)S(1)} %add.2), channel_id=1, replica_groups={{0,2,4,6,8,10,12,14,16,18,20,22,24,26,28,30},{1,3,5,7,9,11,13,15,17,19,..., dimensions={0} | all-to-all | bytes 524288 | tf_op jit(solution)/shard_map/all_to_all | solution.py:446
  60.3 0.0 copy-done.1
  60.3 0.1 shift.1
  60.4 12.8 %all_to_all.22 = bf16[16,64,128]{2,1,0:T(8,128)(2,1)S(1)} all-to-all(bf16[16,64,128]{2,1,0:T(8,128)(2,1)S(1)} %get-tuple-element.9), channel_id=1, replica_groups={{0,2,4,6,8,10,12,14,16,18,20,22,24,26,28,30},{1,3,5,7,9,11,13,15,17,19,..., dimensions={0} | all-to-all | bytes 524288 | tf_op jit(solution)/shard_map/all_to_all | solution.py:448
  73.3 0.0 copy-start.2
  73.3 0.0 collective-permute-start.4
  73.3 1.5 %collective-permute-done.4.other_ref = bf16[1024,128]{1,0:T(8,128)(2,1)S(1)} collective-permute-done((bf16[1024,128]{1,0:T(8,128)(2,1)S(1)}, bf16[1024,128]{1,0:T(8,128)(2,1)S(1)}, u32[]{:S(2)}, u32[]{:S(2)}) %collective-permute-start.4) | collective-permute-done | bytes 262176 | tf_op jit(solution)/shard_map/ppermute | solution.py:449
  74.8 0.0 copy-start.3
  74.8 0.0 copy-done.2
  74.8 0.7 copy-done.3
  75.5 0.0 copy-start
  75.5 22.8 %potential.1 = bf16[32,2,64,128]{3,2,1,0:T(8,128)(2,1)} custom-call(s32[1]{0:T(128)} %bitcast.core_ref, bf16[1024,128]{1,0:T(8,128)(2,1)} %bitcast.11, bf16[1024,128]{1,0:T(8,128)(2,1)} %copy-done.3, bf16[6144,4096]{1,0:T(8,128)(2,1)S(1)} %get-tuple-element.10.kept_ref, bf16[8192,4096]{1,0:T(8,128)(2,1)} %bitcast.3.slab_ref.refs_6_), custom_call_target="tpu_custom_call" | custom-call | flops 4294967296 | bytes 67108864 | tf_op jit(solution)/shard_map/potential/pallas_call | solution.py:355
  98.3 2.7 %all-to-all-start.3 = ((bf16[32,2,64,128]{3,2,1,0:T(8,128)(2,1)}), bf16[32,2,64,128]{3,2,1,0:T(8,128)(2,1)S(1)}, u32[]{:S(2)}, u32[]{:S(2)}) async-start(bf16[32,2,64,128]{3,2,1,0:T(8,128)(2,1)} %potential.1), calls=%async_computation.3 | async-start | bytes 2097152 | tf_op jit(solution)/shard_map/all_to_all | solution.py:450
  101.0 0.6 slice_reduce_fusion
  101.6 26.8 %all-to-all-done.3.refs_0_ = bf16[32,2,64,128]{3,2,1,0:T(8,128)(2,1)S(1)} async-done(((bf16[32,2,64,128]{3,2,1,0:T(8,128)(2,1)}), bf16[32,2,64,128]{3,2,1,0:T(8,128)(2,1)S(1)}, u32[]{:S(2)}, u32[]{:S(2)}) %all-to-all-start.3) | async-done | bytes 1048608 | tf_op jit(solution)/shard_map/all_to_all | solution.py:450
  128.4 0.0 copy-done
  128.4 2.8 %series.1 = f32[2,64,512]{2,1,0:T(8,128)} custom-call(f32[2,64,512]{2,1,0:T(8,128)S(1)} %copy-done, bf16[32,2,64,128]{3,2,1,0:T(8,128)(2,1)S(1)} %all-to-all-done.3.refs_0_), custom_call_target="tpu_custom_call" | custom-call | tf_op jit(solution)/shard_map/series/pallas_call | solution.py:408
Async XLA Ops:
  15.2 9.5 %collective-permute-start.2 = (bf16[512,128]{1,0:T(8,128)(2,1)S(1)}, bf16[512,128]{1,0:T(8,128)(2,1)S(1)}, u32[]{:S(2)}, u32[]{:S(2)}) collective-permute-start(bf16[512,128]{1,0:T(8,128)(2,1)S(1)} %bitcast.5), channel_id=1, source_target_pairs={{0,24},{8,16},{16,8},{24,0},{1,25},{9,17},{17,9},{25,1},{2,26},{10... | collective-permute-start | bytes 393224 | tf_op jit(solution)/shard_map/ppermute | solution.py:437
  17.7 7.0 %collective-permute-start.1 = (bf16[512,128]{1,0:T(8,128)(2,1)S(1)}, bf16[512,128]{1,0:T(8,128)(2,1)S(1)}, u32[]{:S(2)}, u32[]{:S(2)}) collective-permute-start(bf16[512,128]{1,0:T(8,128)(2,1)S(1)} %bitcast.6), channel_id=1, source_target_pairs={{0,16},{8,24},{16,0},{24,8},{1,17},{9,25},{17,1},{25,9},{2,18},{10... | collective-permute-start | bytes 393224 | tf_op jit(solution)/shard_map/ppermute | solution.py:437
  18.2 6.5 %collective-permute-start = (bf16[512,128]{1,0:T(8,128)(2,1)S(1)}, bf16[512,128]{1,0:T(8,128)(2,1)S(1)}, u32[]{:S(2)}, u32[]{:S(2)}) collective-permute-start(bf16[512,128]{1,0:T(8,128)(2,1)S(1)} %bitcast.7), channel_id=1, source_target_pairs={{0,8},{8,0},{16,24},{24,16},{1,9},{9,1},{17,25},{25,17},{2,10},{10... | collective-permute-start | bytes 393224 | tf_op jit(solution)/shard_map/ppermute | solution.py:437
  24.7 35.6 %copy-start.1 = (f32[2,4096]{1,0:T(2,128)S(1)}, f32[2,4096]{1,0:T(2,128)}, u32[]{:S(2)}) copy-start(f32[2,4096]{1,0:T(2,128)} %fields_ref.1) | copy-start | bytes 98308
  43.0 1.8 %collective-permute-start.3 = (bf16[16,64,128]{2,1,0:T(8,128)(2,1)}, bf16[16,64,128]{2,1,0:T(8,128)(2,1)S(1)}, u32[]{:S(2)}, u32[]{:S(2)}) collective-permute-start(bf16[16,64,128]{2,1,0:T(8,128)(2,1)} %get-tuple-element.8), channel_id=1, source_target_pairs={{0,1},{1,0},{2,3},{3,2},{4,5},{5,4},{6,7},{7,6},{8,9},{9,8},{10,11... | collective-permute-start | bytes 786440 | tf_op jit(solution)/shard_map/ppermute | solution.py:446
  73.3 1.5 %copy-start.2 = (bf16[16,64,128]{2,1,0:T(8,128)(2,1)}, bf16[16,64,128]{2,1,0:T(8,128)(2,1)S(1)}, u32[]{:S(2)}) copy-start(bf16[16,64,128]{2,1,0:T(8,128)(2,1)S(1)} %all_to_all.22) | copy-start | bytes 786436
  73.3 1.5 %collective-permute-start.4 = (bf16[1024,128]{1,0:T(8,128)(2,1)S(1)}, bf16[1024,128]{1,0:T(8,128)(2,1)S(1)}, u32[]{:S(2)}, u32[]{:S(2)}) collective-permute-start(bf16[1024,128]{1,0:T(8,128)(2,1)S(1)} %bitcast.10), channel_id=1, source_target_pairs={{0,1},{1,0},{2,3},{3,2},{4,5},{5,4},{6,7},{7,6},{8,9},{9,8},{10,11... | collective-permute-start | bytes 786440 | tf_op jit(solution)/shard_map/ppermute | solution.py:449
  74.8 0.7 copy-start.3
  75.5 52.9 %copy-start = (f32[2,64,512]{2,1,0:T(8,128)S(1)}, f32[2,64,512]{2,1,0:T(8,128)}, u32[]{:S(2)}) copy-start(f32[2,64,512]{2,1,0:T(8,128)} %walkers_ref.1) | copy-start | bytes 786436
  98.3 30.1 %all-to-all-start.3 = ((bf16[32,2,64,128]{3,2,1,0:T(8,128)(2,1)}), bf16[32,2,64,128]{3,2,1,0:T(8,128)(2,1)S(1)}, u32[]{:S(2)}, u32[]{:S(2)}) async-start(bf16[32,2,64,128]{3,2,1,0:T(8,128)(2,1)} %potential.1), calls=%async_computation.3 | async-start | bytes 2097152 | tf_op jit(solution)/shard_map/all_to_all | solution.py:450
